TPU v7x, 32 devices: a whole 2x2x4 slice. The times are simulated.
32 devices in a mesh: cases: 2 (over x), box: 16 (over z, y, core).
Axes of the slice: x: 2, y: 2, z: 4, core: 2. Of those that a mesh axis runs over, the one named last changes fastest.
Arguments:
- positions: float32 [2048, 3, 128], P(('cases', 'box')), parts along dimension 0, may hold values from -9 to 9, as said below
- strengths: float32 [2048, 3, 128], P(('cases', 'box')), parts along dimension 0, may hold values from -12 to 12
- history: float32 [2048, 2, 3, 128], P(('cases', 'box')), parts along dimension 0, may hold values from -5 to 5
- move_list: int32 [2048], P(('cases', 'box')), parts along dimension 0, may hold values from 0 to 1023, as said below
- age_slot: int32 [2048], P(('cases', 'box')), parts along dimension 0, may hold values from 0 to 1023, as said below
- fetch_list: int32 [32, 16, 8], P(('cases', 'box')), parts along dimension 0, may hold values from -1 to 63, as said below
- tile_slot: int32 [2048, 32], P(('cases', 'box')), parts along dimension 0, may hold values from 0 to 127, as said below
- tile_count: int32 [2048], P(('cases', 'box')), parts along dimension 0, may hold values from 1 to 32, as said below
- blade_id: int32 [2048, 128], P(('cases', 'box')), parts along dimension 0, may hold values from 0 to 17
- hub_centre: float32 [12, 3], P('cases'), parts along dimension 0, may hold values from -8 to 8
- azimuth: float32 [12], P('cases'), parts along dimension 0, may hold values from -3.140625 to 3.140625
Outputs:
- new_positions: float32 [2048, 3, 128], P(('cases', 'box')), parts along dimension 0
- new_history: float32 [2048, 2, 3, 128], P(('cases', 'box')), parts along dimension 0
- frame: float32 [2048, 3, 128], P(('cases', 'box')), parts along dimension 0
There are 2 independent parts, one for each index of `cases`. A program takes and returns all parts, laid end to end along the dimension named above; each array names one. Nothing has to cross between parts.
Inputs may be any that keep to these rules, and one draw needn't show every extreme that they name: Node positions; the first component of a block's nodes is offset by an amount that grows with the block's device. `move_list`: A permutation of block ids (block id = device * 64 + local block). Each device receives 64 blocks; the blocks of one device go at most 8 to any one device, and every device sends exactly 8 to some device. `age_slot`: A permutation of block ids, with the same bounds per pair of devices as move_list. `fetch_list`: entry [r, o, i] is -1 or a local block of device o; live entries come first in each [r, o] row and are distinct; rows [r, o] with o within two of r around the axis have 8 live entries. `tile_slot`: every entry names a live entry of fetch_list for the target block's device; tiles may repeat. `tile_count`: the first block of each device has 32.
All inputs are finite; a program needn't handle non-finite values.
Results may differ from a plain program's by a relative error of at most 0.0003.
Values sent between devices are 32-bit elements; how exact they have to be, the bound alone decides.
No kernel may reach another device: no remote copies, remote signals or barrier semaphores. Data moves between devices by JAX's collectives and lax.ppermute only.
A program may use at most 128 MiB of HBM per device.

v0:
```python
import math

import jax
import jax.numpy as jnp
from jax import lax
from jax.sharding import PartitionSpec as P

ROTORS = 6
BLADES = 3


core_square = 0.05
time_step = 0.05


def cross_product(first, second):
    return jnp.stack(
        [
            first[..., 1, :] * second[..., 2, :] - first[..., 2, :] * second[..., 1, :],
            first[..., 2, :] * second[..., 0, :] - first[..., 0, :] * second[..., 2, :],
            first[..., 0, :] * second[..., 1, :] - first[..., 1, :] * second[..., 0, :],
        ],
        axis=-2,
    )


def induced(target, source_pos, source_table, tile_mask):
    dist_sq = jnp.zeros((source_pos.shape[0], target.shape[-1], source_pos.shape[-1]), jnp.float32)
    for component in range(3):
        gap = target[component][None, :, None] - source_pos[:, component][:, None, :]
        dist_sq = dist_sq + gap * gap
    weight = tile_mask[:, None, None] * (dist_sq + core_square) ** (-1.5)
    summed = jnp.einsum("kij,kcj->ci", weight, source_table, precision=lax.Precision.HIGHEST)
    return (cross_product(target, summed[:3]) - summed[3:]) / (4.0 * math.pi)


def pack_blocks(values, targets, blocks, box_count, capacity):
    dest_box = targets // blocks
    dest_local = targets % blocks
    one_hot = (dest_box[:, None] == jnp.arange(box_count, dtype=jnp.int32)[None, :]).astype(
        jnp.int32
    )
    earlier = jnp.cumsum(one_hot, axis=0) - one_hot
    ranking = jnp.sum(earlier * one_hot, axis=1)
    place = dest_box * capacity + ranking
    buffer = (
        jnp.zeros((box_count * capacity,) + values.shape[1:], values.dtype).at[place].set(values)
    )
    labels = (
        jnp.full((box_count * capacity,), -1.0, jnp.float32)
        .at[place]
        .set(dest_local.astype(jnp.float32))
    )
    return (buffer, labels)


def unpack_blocks(arrived, labels, blocks):
    place = jnp.where(labels >= 0.0, labels, float(blocks)).astype(jnp.int32)
    return (
        jnp.zeros((blocks,) + arrived.shape[1:], arrived.dtype).at[place].set(arrived, mode="drop")
    )


def body(
    positions,
    strengths,
    history,
    move_list,
    age_slot,
    fetch_list,
    tile_slot,
    tile_count,
    blade_id,
    hub_centre,
    azimuth,
):
    blocks = positions.shape[0]
    box_count = lax.axis_size("box")
    capacity = 2 * blocks // box_count
    offered = jnp.concatenate([positions, strengths], axis=1)
    requests = fetch_list[0]
    everything = lax.all_gather(offered, "box", axis=0, tiled=True)
    wanted = jnp.arange(box_count, dtype=jnp.int32)[:, None] * blocks + jnp.clip(
        requests, 0, blocks - 1
    )
    fetched = jnp.take(everything, wanted.reshape(-1), axis=0)
    source_pos = fetched[:, :3]
    source_table = jnp.concatenate(
        [fetched[:, 3:], cross_product(fetched[:, :3], fetched[:, 3:])], axis=1
    )
    tile_mask = (
        jnp.arange(tile_slot.shape[1], dtype=jnp.int32)[None, :] < tile_count[:, None]
    ).astype(jnp.float32)

    def one_target(packed):
        target, slots, weights = packed
        return induced(
            target,
            jnp.take(source_pos, slots, axis=0),
            jnp.take(source_table, slots, axis=0),
            weights,
        )

    velocity = lax.map(one_target, (positions, tile_slot, tile_mask), batch_size=4)
    buffer, labels = pack_blocks(history, move_list, blocks, box_count, capacity)
    arrived, arrived_labels = (
        lax.all_to_all(buffer, "box", split_axis=0, concat_axis=0, tiled=True),
        lax.all_to_all(labels, "box", split_axis=0, concat_axis=0, tiled=True),
    )
    moved = unpack_blocks(arrived, arrived_labels, blocks)
    new_positions = (
        positions + time_step * (23.0 * velocity - 16.0 * moved[:, 0] + 5.0 * moved[:, 1]) / 12.0
    )
    new_history = jnp.stack([velocity, moved[:, 0]], axis=1)
    age_buffer, age_labels = pack_blocks(new_positions, age_slot, blocks, box_count, capacity)
    aged_in, aged_labels = (
        lax.all_to_all(age_buffer, "box", split_axis=0, concat_axis=0, tiled=True),
        lax.all_to_all(age_labels, "box", split_axis=0, concat_axis=0, tiled=True),
    )
    aged = unpack_blocks(aged_in, aged_labels, blocks)
    classes = ROTORS * BLADES
    blade_angle = (
        azimuth[:, None] + 2.0 * math.pi * jnp.arange(BLADES, dtype=jnp.float32)[None, :] / BLADES
    ).reshape(-1)
    centre_table = jnp.repeat(hub_centre, BLADES, axis=0)
    selector = (blade_id[None, :, :] == jnp.arange(classes, dtype=jnp.int32)[:, None, None]).astype(
        jnp.float32
    )
    cosine = jnp.sum(selector * jnp.cos(blade_angle)[:, None, None], axis=0)
    sine = jnp.sum(selector * jnp.sin(blade_angle)[:, None, None], axis=0)
    first = aged[:, 0] - jnp.sum(selector * centre_table[:, 0][:, None, None], axis=0)
    second = aged[:, 1] - jnp.sum(selector * centre_table[:, 1][:, None, None], axis=0)
    third = aged[:, 2] - jnp.sum(selector * centre_table[:, 2][:, None, None], axis=0)
    frame = jnp.stack(
        [cosine * first + sine * second, cosine * second - sine * first, third], axis=1
    )
    return (new_positions, new_history, frame)


def solution(mesh):
    placed = (
        P(("cases", "box"), None, None),
        P(("cases", "box"), None, None),
        P(("cases", "box"), None, None, None),
        P(("cases", "box")),
        P(("cases", "box")),
        P(("cases", "box"), None, None),
        P(("cases", "box"), None),
        P(("cases", "box")),
        P(("cases", "box"), None),
        P("cases", None),
        P("cases"),
    )
    return jax.shard_map(
        body,
        mesh=mesh,
        in_specs=placed,
        out_specs=(
            P(("cases", "box"), None, None),
            P(("cases", "box"), None, None, None),
            P(("cases", "box"), None, None),
        ),
        check_vma=False,
    )
```

profile of v0, /device:TPU:0, one launch (start us, length us, event | category | flops | bytes accessed | tf_op | source)
XLA Modules:
  0.0 342.8 jit_solution(4448846752251217391)
XLA Ops:
  7.2 1.6 pad_maximum_fusion.1
  11.4 7.4 %all-to-all-start = ((f32[16,8,1]{1,2,0:T(1,128)}), f32[16,8,1]{1,2,0:T(1,128)S(1)}, u32[]{:S(2)}, u32[]{:S(2)}) async-start(f32[16,8,1]{1,2,0:T(1,128)} %bitcast.25), calls=%async_computation | async-start | bytes 16384 | tf_op jit(solution)/shard_map/all_to_all | solution.py:108
  25.8 0.8 broadcast_in_dim.87
  26.7 8.0 %scatter_fusion = f32[128,2,3,128]{3,1,2,0:T(2,128)} fusion(f32[128,2,3,128]{3,1,2,0:T(2,128)} %broadcast_in_dim.87, s32[64]{0:T(128)S(1)} %compare_select_fusion.7, f32[64,2,3,128]{3,1,2,0:T(2,128)} %param.15), kind=kCustom, calls=%fused_computation.4 | custom fusion | bytes 590080 | tf_op jit(solution)/shard_map/scatter | solution.py:47
  34.7 6.0 %all-to-all-start.1 = ((f32[128,2,3,128]{3,1,2,0:T(2,128)}), f32[128,2,3,128]{3,1,2,0:T(2,128)S(1)}, u32[]{:S(2)}, u32[]{:S(2)}) async-start(f32[128,2,3,128]{3,1,2,0:T(2,128)} %scatter_fusion), calls=%async_computation.1 | async-start | bytes 786432 | tf_op jit(solution)/shard_map/all_to_all | solution.py:107
  42.1 17.4 %all-to-all-done.1 = f32[128,2,3,128]{3,1,2,0:T(2,128)S(1)} async-done(((f32[128,2,3,128]{3,1,2,0:T(2,128)}), f32[128,2,3,128]{3,1,2,0:T(2,128)S(1)}, u32[]{:S(2)}, u32[]{:S(2)}) %all-to-all-start.1) | async-done | bytes 393248 | tf_op jit(solution)/shard_map/all_to_all | solution.py:107
  59.5 6.3 %all-to-all-start.2 = ((f32[16,8,1]{1,2,0:T(1,128)}), f32[16,8,1]{1,2,0:T(1,128)S(1)}, u32[]{:S(2)}, u32[]{:S(2)}) async-start(f32[16,8,1]{1,2,0:T(1,128)} %bitcast.31), calls=%async_computation.2 | async-start | bytes 16384 | tf_op jit(solution)/shard_map/all_to_all | solution.py:118
  65.8 4.7 %scatter_fusion.1 = f32[64,2,3,128]{3,1,2,0:T(2,128)S(1)} fusion(f32[64,2,3,128]{3,1,2,0:T(2,128)S(1)} %broadcast_in_dim.84, s32[128]{0:T(128)S(1)} %fusion.44, f32[128,2,3,128]{3,1,2,0:T(2,128)S(1)} %all-to-all-done.1), kind=kCustom, calls=%fused_computation.5 | custom fusion | bytes 1180160 | tf_op jit(solution)/shard_map/scatter | solution.py:60
  70.7 5.7 %copy.106 = f32[1024,6,128]{2,1,0:T(8,128)} copy(f32[1024,6,128]{2,0,1:T(8,128)} %all-gather.2.cloned.1.call-done) | data formatting | bytes 6291456 | tf_op jit(solution)/shard_map/all_gather | solution.py:82
  76.4 2.9 gather_fusion.2
  80.2 226.8 %while.10 = (s32[]{:T(128)}, f32[16,4,3,128]{3,2,1,0:T(4,128)S(1)}, f32[16,4,3,128]{3,1,0,2:T(4,128)S(1)}, s32[16,4,32]{2,1,0:T(4,128)S(1)}, f32[128,6,128]{2,1,...) while((s32[]{:T(128)}, f32[16,4,3,128]{3,2,1,0:T(4,128)S(1)}, ...), condition=%wide.region_1.2_spmd, body=%wide.region_0.1_spmd.sunk | while | flops 172126848 | bytes 2662377 | solution.py:104
  82.4 12.0 %fusion.64 = f32[4,6,128]{2,1,0:T(8,128)S(1)} fusion(f32[4,32,128]{2,1,0:T(8,128)S(1)} %bitcast.126, f32[4,128]{1,0:T(4,128)S(1)} %get-tuple-element.200, f32[4,32,128]{2,1,0:T(8,128)S(1)} %bitcast.127, f32[4,128]{1,0:T(4,128)S(1)} %get-tuple-element.202, f32[4,32,128]{2,1,0:T(8,128)S(1)} %bitcast.125, f32[4,128]{1,0:T(4,128)S(1)} %get-tuple-element.204, ...), kind=kOutput, calls=%fused_computation.30.clone.1 | convolution fusion | flops 172064768 | bytes 608896 | tf_op jit(solution)/shard_map/while/body/eval_jaxpr/vmap(kij,kcj->ci)/dot_general | solution.py:33
  96.6 12.0 %fusion.64 = f32[4,6,128]{2,1,0:T(8,128)S(1)} fusion(f32[4,32,128]{2,1,0:T(8,128)S(1)} %bitcast.126, f32[4,128]{1,0:T(4,128)S(1)} %get-tuple-element.200, f32[4,32,128]{2,1,0:T(8,128)S(1)} %bitcast.127, f32[4,128]{1,0:T(4,128)S(1)} %get-tuple-element.202, f32[4,32,128]{2,1,0:T(8,128)S(1)} %bitcast.125, f32[4,128]{1,0:T(4,128)S(1)} %get-tuple-element.204, ...), kind=kOutput, calls=%fused_computation.30.clone.1 | convolution fusion | flops 172064768 | bytes 608896 | tf_op jit(solution)/shard_map/while/body/eval_jaxpr/vmap(kij,kcj->ci)/dot_general | solution.py:33
  110.8 12.0 %fusion.64 = f32[4,6,128]{2,1,0:T(8,128)S(1)} fusion(f32[4,32,128]{2,1,0:T(8,128)S(1)} %bitcast.126, f32[4,128]{1,0:T(4,128)S(1)} %get-tuple-element.200, f32[4,32,128]{2,1,0:T(8,128)S(1)} %bitcast.127, f32[4,128]{1,0:T(4,128)S(1)} %get-tuple-element.202, f32[4,32,128]{2,1,0:T(8,128)S(1)} %bitcast.125, f32[4,128]{1,0:T(4,128)S(1)} %get-tuple-element.204, ...), kind=kOutput, calls=%fused_computation.30.clone.1 | convolution fusion | flops 172064768 | bytes 608896 | tf_op jit(solution)/shard_map/while/body/eval_jaxpr/vmap(kij,kcj->ci)/dot_general | solution.py:33
  124.9 12.0 %fusion.64 = f32[4,6,128]{2,1,0:T(8,128)S(1)} fusion(f32[4,32,128]{2,1,0:T(8,128)S(1)} %bitcast.126, f32[4,128]{1,0:T(4,128)S(1)} %get-tuple-element.200, f32[4,32,128]{2,1,0:T(8,128)S(1)} %bitcast.127, f32[4,128]{1,0:T(4,128)S(1)} %get-tuple-element.202, f32[4,32,128]{2,1,0:T(8,128)S(1)} %bitcast.125, f32[4,128]{1,0:T(4,128)S(1)} %get-tuple-element.204, ...), kind=kOutput, calls=%fused_computation.30.clone.1 | convolution fusion | flops 172064768 | bytes 608896 | tf_op jit(solution)/shard_map/while/body/eval_jaxpr/vmap(kij,kcj->ci)/dot_general | solution.py:33
  139.1 12.0 %fusion.64 = f32[4,6,128]{2,1,0:T(8,128)S(1)} fusion(f32[4,32,128]{2,1,0:T(8,128)S(1)} %bitcast.126, f32[4,128]{1,0:T(4,128)S(1)} %get-tuple-element.200, f32[4,32,128]{2,1,0:T(8,128)S(1)} %bitcast.127, f32[4,128]{1,0:T(4,128)S(1)} %get-tuple-element.202, f32[4,32,128]{2,1,0:T(8,128)S(1)} %bitcast.125, f32[4,128]{1,0:T(4,128)S(1)} %get-tuple-element.204, ...), kind=kOutput, calls=%fused_computation.30.clone.1 | convolution fusion | flops 172064768 | bytes 608896 | tf_op jit(solution)/shard_map/while/body/eval_jaxpr/vmap(kij,kcj->ci)/dot_general | solution.py:33
  153.3 12.0 %fusion.64 = f32[4,6,128]{2,1,0:T(8,128)S(1)} fusion(f32[4,32,128]{2,1,0:T(8,128)S(1)} %bitcast.126, f32[4,128]{1,0:T(4,128)S(1)} %get-tuple-element.200, f32[4,32,128]{2,1,0:T(8,128)S(1)} %bitcast.127, f32[4,128]{1,0:T(4,128)S(1)} %get-tuple-element.202, f32[4,32,128]{2,1,0:T(8,128)S(1)} %bitcast.125, f32[4,128]{1,0:T(4,128)S(1)} %get-tuple-element.204, ...), kind=kOutput, calls=%fused_computation.30.clone.1 | convolution fusion | flops 172064768 | bytes 608896 | tf_op jit(solution)/shard_map/while/body/eval_jaxpr/vmap(kij,kcj->ci)/dot_general | solution.py:33
  167.4 12.0 %fusion.64 = f32[4,6,128]{2,1,0:T(8,128)S(1)} fusion(f32[4,32,128]{2,1,0:T(8,128)S(1)} %bitcast.126, f32[4,128]{1,0:T(4,128)S(1)} %get-tuple-element.200, f32[4,32,128]{2,1,0:T(8,128)S(1)} %bitcast.127, f32[4,128]{1,0:T(4,128)S(1)} %get-tuple-element.202, f32[4,32,128]{2,1,0:T(8,128)S(1)} %bitcast.125, f32[4,128]{1,0:T(4,128)S(1)} %get-tuple-element.204, ...), kind=kOutput, calls=%fused_computation.30.clone.1 | convolution fusion | flops 172064768 | bytes 608896 | tf_op jit(solution)/shard_map/while/body/eval_jaxpr/vmap(kij,kcj->ci)/dot_general | solution.py:33
  181.6 12.0 %fusion.64 = f32[4,6,128]{2,1,0:T(8,128)S(1)} fusion(f32[4,32,128]{2,1,0:T(8,128)S(1)} %bitcast.126, f32[4,128]{1,0:T(4,128)S(1)} %get-tuple-element.200, f32[4,32,128]{2,1,0:T(8,128)S(1)} %bitcast.127, f32[4,128]{1,0:T(4,128)S(1)} %get-tuple-element.202, f32[4,32,128]{2,1,0:T(8,128)S(1)} %bitcast.125, f32[4,128]{1,0:T(4,128)S(1)} %get-tuple-element.204, ...), kind=kOutput, calls=%fused_computation.30.clone.1 | convolution fusion | flops 172064768 | bytes 608896 | tf_op jit(solution)/shard_map/while/body/eval_jaxpr/vmap(kij,kcj->ci)/dot_general | solution.py:33
  195.8 12.0 %fusion.64 = f32[4,6,128]{2,1,0:T(8,128)S(1)} fusion(f32[4,32,128]{2,1,0:T(8,128)S(1)} %bitcast.126, f32[4,128]{1,0:T(4,128)S(1)} %get-tuple-element.200, f32[4,32,128]{2,1,0:T(8,128)S(1)} %bitcast.127, f32[4,128]{1,0:T(4,128)S(1)} %get-tuple-element.202, f32[4,32,128]{2,1,0:T(8,128)S(1)} %bitcast.125, f32[4,128]{1,0:T(4,128)S(1)} %get-tuple-element.204, ...), kind=kOutput, calls=%fused_computation.30.clone.1 | convolution fusion | flops 172064768 | bytes 608896 | tf_op jit(solution)/shard_map/while/body/eval_jaxpr/vmap(kij,kcj->ci)/dot_general | solution.py:33
  209.9 12.0 %fusion.64 = f32[4,6,128]{2,1,0:T(8,128)S(1)} fusion(f32[4,32,128]{2,1,0:T(8,128)S(1)} %bitcast.126, f32[4,128]{1,0:T(4,128)S(1)} %get-tuple-element.200, f32[4,32,128]{2,1,0:T(8,128)S(1)} %bitcast.127, f32[4,128]{1,0:T(4,128)S(1)} %get-tuple-element.202, f32[4,32,128]{2,1,0:T(8,128)S(1)} %bitcast.125, f32[4,128]{1,0:T(4,128)S(1)} %get-tuple-element.204, ...), kind=kOutput, calls=%fused_computation.30.clone.1 | convolution fusion | flops 172064768 | bytes 608896 | tf_op jit(solution)/shard_map/while/body/eval_jaxpr/vmap(kij,kcj->ci)/dot_general | solution.py:33
  224.1 12.0 %fusion.64 = f32[4,6,128]{2,1,0:T(8,128)S(1)} fusion(f32[4,32,128]{2,1,0:T(8,128)S(1)} %bitcast.126, f32[4,128]{1,0:T(4,128)S(1)} %get-tuple-element.200, f32[4,32,128]{2,1,0:T(8,128)S(1)} %bitcast.127, f32[4,128]{1,0:T(4,128)S(1)} %get-tuple-element.202, f32[4,32,128]{2,1,0:T(8,128)S(1)} %bitcast.125, f32[4,128]{1,0:T(4,128)S(1)} %get-tuple-element.204, ...), kind=kOutput, calls=%fused_computation.30.clone.1 | convolution fusion | flops 172064768 | bytes 608896 | tf_op jit(solution)/shard_map/while/body/eval_jaxpr/vmap(kij,kcj->ci)/dot_general | solution.py:33
  238.2 12.0 %fusion.64 = f32[4,6,128]{2,1,0:T(8,128)S(1)} fusion(f32[4,32,128]{2,1,0:T(8,128)S(1)} %bitcast.126, f32[4,128]{1,0:T(4,128)S(1)} %get-tuple-element.200, f32[4,32,128]{2,1,0:T(8,128)S(1)} %bitcast.127, f32[4,128]{1,0:T(4,128)S(1)} %get-tuple-element.202, f32[4,32,128]{2,1,0:T(8,128)S(1)} %bitcast.125, f32[4,128]{1,0:T(4,128)S(1)} %get-tuple-element.204, ...), kind=kOutput, calls=%fused_computation.30.clone.1 | convolution fusion | flops 172064768 | bytes 608896 | tf_op jit(solution)/shard_map/while/body/eval_jaxpr/vmap(kij,kcj->ci)/dot_general | solution.py:33
  252.4 12.0 %fusion.64 = f32[4,6,128]{2,1,0:T(8,128)S(1)} fusion(f32[4,32,128]{2,1,0:T(8,128)S(1)} %bitcast.126, f32[4,128]{1,0:T(4,128)S(1)} %get-tuple-element.200, f32[4,32,128]{2,1,0:T(8,128)S(1)} %bitcast.127, f32[4,128]{1,0:T(4,128)S(1)} %get-tuple-element.202, f32[4,32,128]{2,1,0:T(8,128)S(1)} %bitcast.125, f32[4,128]{1,0:T(4,128)S(1)} %get-tuple-element.204, ...), kind=kOutput, calls=%fused_computation.30.clone.1 | convolution fusion | flops 172064768 | bytes 608896 | tf_op jit(solution)/shard_map/while/body/eval_jaxpr/vmap(kij,kcj->ci)/dot_general | solution.py:33
  266.6 12.0 %fusion.64 = f32[4,6,128]{2,1,0:T(8,128)S(1)} fusion(f32[4,32,128]{2,1,0:T(8,128)S(1)} %bitcast.126, f32[4,128]{1,0:T(4,128)S(1)} %get-tuple-element.200, f32[4,32,128]{2,1,0:T(8,128)S(1)} %bitcast.127, f32[4,128]{1,0:T(4,128)S(1)} %get-tuple-element.202, f32[4,32,128]{2,1,0:T(8,128)S(1)} %bitcast.125, f32[4,128]{1,0:T(4,128)S(1)} %get-tuple-element.204, ...), kind=kOutput, calls=%fused_computation.30.clone.1 | convolution fusion | flops 172064768 | bytes 608896 | tf_op jit(solution)/shard_map/while/body/eval_jaxpr/vmap(kij,kcj->ci)/dot_general | solution.py:33
  280.7 12.0 %fusion.64 = f32[4,6,128]{2,1,0:T(8,128)S(1)} fusion(f32[4,32,128]{2,1,0:T(8,128)S(1)} %bitcast.126, f32[4,128]{1,0:T(4,128)S(1)} %get-tuple-element.200, f32[4,32,128]{2,1,0:T(8,128)S(1)} %bitcast.127, f32[4,128]{1,0:T(4,128)S(1)} %get-tuple-element.202, f32[4,32,128]{2,1,0:T(8,128)S(1)} %bitcast.125, f32[4,128]{1,0:T(4,128)S(1)} %get-tuple-element.204, ...), kind=kOutput, calls=%fused_computation.30.clone.1 | convolution fusion | flops 172064768 | bytes 608896 | tf_op jit(solution)/shard_map/while/body/eval_jaxpr/vmap(kij,kcj->ci)/dot_general | solution.py:33
  294.9 12.0 %fusion.64 = f32[4,6,128]{2,1,0:T(8,128)S(1)} fusion(f32[4,32,128]{2,1,0:T(8,128)S(1)} %bitcast.126, f32[4,128]{1,0:T(4,128)S(1)} %get-tuple-element.200, f32[4,32,128]{2,1,0:T(8,128)S(1)} %bitcast.127, f32[4,128]{1,0:T(4,128)S(1)} %get-tuple-element.202, f32[4,32,128]{2,1,0:T(8,128)S(1)} %bitcast.125, f32[4,128]{1,0:T(4,128)S(1)} %get-tuple-element.204, ...), kind=kOutput, calls=%fused_computation.30.clone.1 | convolution fusion | flops 172064768 | bytes 608896 | tf_op jit(solution)/shard_map/while/body/eval_jaxpr/vmap(kij,kcj->ci)/dot_general | solution.py:33
  307.9 6.5 %scatter_fusion.2 = f32[128,3,128]{2,1,0:T(4,128)} fusion(f32[128,3,128]{2,1,0:T(4,128)} %broadcast_in_dim.90, s32[64]{0:T(128)S(1)} %compare_select_fusion.4, f32[64,3,128]{2,1,0:T(4,128)S(1)} %copy.114), kind=kCustom, calls=%fused_computation.7 | custom fusion | bytes 295168 | tf_op jit(solution)/shard_map/scatter | solution.py:47
  314.5 6.0 %all-to-all-start.3 = ((f32[128,3,128]{2,1,0:T(4,128)}), f32[128,3,128]{2,1,0:T(4,128)S(1)}, u32[]{:S(2)}, u32[]{:S(2)}) async-start(f32[128,3,128]{2,1,0:T(4,128)} %scatter_fusion.2), calls=%async_computation.3 | async-start | bytes 524288 | tf_op jit(solution)/shard_map/all_to_all | solution.py:117
  321.6 0.8 copy.115
  322.5 8.1 %all-to-all-done.3 = f32[128,3,128]{2,1,0:T(4,128)S(1)} async-done(((f32[128,3,128]{2,1,0:T(4,128)}), f32[128,3,128]{2,1,0:T(4,128)S(1)}, u32[]{:S(2)}, u32[]{:S(2)}) %all-to-all-start.3) | async-done | bytes 196640 | tf_op jit(solution)/shard_map/all_to_all | solution.py:117
  330.6 4.5 %scatter_fusion.3 = f32[64,3,128]{2,1,0:T(4,128)S(1)} fusion(f32[64,3,128]{2,1,0:T(4,128)S(1)} %broadcast_in_dim.88, s32[128]{0:T(128)S(1)} %fusion.46, f32[128,3,128]{2,1,0:T(4,128)S(1)} %all-to-all-done.3), kind=kCustom, calls=%fused_computation.8 | custom fusion | bytes 590336 | tf_op jit(solution)/shard_map/scatter | solution.py:60
  (297 shorter events, 47.7 us)
Async XLA Ops:
  7.2 63.5 %all-gather.2.cloned.1.call-start = ((), (), s32[]{:S(2)}) async-start(), calls=%async_computation.4 | async-start | bytes 3342336 | tf_op jit(solution)/shard_map/all_gather | solution.py:82
  11.4 23.3 %all-to-all-start = ((f32[16,8,1]{1,2,0:T(1,128)}), f32[16,8,1]{1,2,0:T(1,128)S(1)}, u32[]{:S(2)}, u32[]{:S(2)}) async-start(f32[16,8,1]{1,2,0:T(1,128)} %bitcast.25), calls=%async_computation | async-start | bytes 16384 | tf_op jit(solution)/shard_map/all_to_all | solution.py:108
  34.7 24.8 %all-to-all-start.1 = ((f32[128,2,3,128]{3,1,2,0:T(2,128)}), f32[128,2,3,128]{3,1,2,0:T(2,128)S(1)}, u32[]{:S(2)}, u32[]{:S(2)}) async-start(f32[128,2,3,128]{3,1,2,0:T(2,128)} %scatter_fusion), calls=%async_computation.1 | async-start | bytes 786432 | tf_op jit(solution)/shard_map/all_to_all | solution.py:107
  59.5 255.0 %all-to-all-start.2 = ((f32[16,8,1]{1,2,0:T(1,128)}), f32[16,8,1]{1,2,0:T(1,128)S(1)}, u32[]{:S(2)}, u32[]{:S(2)}) async-start(f32[16,8,1]{1,2,0:T(1,128)} %bitcast.31), calls=%async_computation.2 | async-start | bytes 16384 | tf_op jit(solution)/shard_map/all_to_all | solution.py:118
  76.4 3.8 %copy-start = (f32[64,3,128]{2,0,1:T(8,128)S(1)}, f32[64,3,128]{2,0,1:T(8,128)}, u32[]{:S(2)}) copy-start(f32[64,3,128]{2,0,1:T(8,128)} %param.13) | copy-start | bytes 294916
  80.2 240.3 %copy-start.2 = (s32[64,128]{1,0:T(8,128)S(1)}, s32[64,128]{1,0:T(8,128)}, u32[]{:S(2)}) copy-start(s32[64,128]{1,0:T(8,128)} %param.21) | copy-start | bytes 98308
  307.1 28.8 %copy-start.1 = (f32[64,3,128]{2,0,1:T(8,128)}, f32[64,3,128]{2,0,1:T(8,128)S(1)}, u32[]{:S(2)}) copy-start(f32[64,3,128]{2,0,1:T(8,128)S(1)} %fusion.36) | copy-start | bytes 294916
  314.5 16.1 %all-to-all-start.3 = ((f32[128,3,128]{2,1,0:T(4,128)}), f32[128,3,128]{2,1,0:T(4,128)S(1)}, u32[]{:S(2)}, u32[]{:S(2)}) async-start(f32[128,3,128]{2,1,0:T(4,128)} %scatter_fusion.2), calls=%async_computation.3 | async-start | bytes 524288 | tf_op jit(solution)/shard_map/all_to_all | solution.py:117
Sparse Core Ops, SparseCore 0:
  10.8 54.3 all-gather.1
where the time goes:
time: 344 us; the launch traced here: 343 us
  matrix products  192 us (56%)
  local copies, waits for them, and re-layouts  70.9 us (21%)
  starting transfers between devices  25.7 us (7%)
  waiting for transfers between devices  25.5 us (7%)
  between operations  14.4 us (4%)
  other arithmetic  12.3 us (4%)
    dot_general x16, matrix products, induced(): jnp.einsum('kij,kcj->ci', weight, source_table, precision=lax.Precision.H...  192 us
    all_to_all x1, waiting for transfers between devices, body(): lax.all_to_all(buffer, 'box', split_axis=0, concat_axis=0, tiled=True)  17.4 us
    scatter x2, local copies, waits for them, and re-layouts, pack_blocks(): jnp.zeros((box_count * capacity,) + values.shape[1:], values.dtype)  14.5 us
    gather x16, local copies, waits for them, and re-layouts, one_target(): jnp.take(source_table, slots, axis=0)  12.2 us
    gather x16, local copies, waits for them, and re-layouts, one_target(): jnp.take(source_pos, slots, axis=0)  12 us
    scatter x2, local copies, waits for them, and re-layouts, unpack_blocks(): jnp.zeros((blocks,) + arrived.shape[1:], arrived.dtype).at[place]  9.19 us
    all_to_all x1, waiting for transfers between devices, body(): lax.all_to_all(age_buffer, 'box', split_axis=0, concat_axis=0, tiled=True)  8.07 us
    all_to_all x1, starting transfers between devices, body(): lax.all_to_all(labels, 'box', split_axis=0, concat_axis=0, tiled=True)  7.39 us
  transfers between devices with their start and end apart: 5, of which 2 were waited for; matrix products, arithmetic and copies ran while one was open for 78% of the time, Pallas kernels for 0%

commit v1 on v0

v1 whole, which is shorter than its diff:
```python
import functools
import math

import jax
import jax.numpy as jnp
from jax import lax
from jax.experimental import pallas as pl
from jax.experimental.pallas import tpu as pltpu
from jax.sharding import PartitionSpec as P

ROTORS = 6
BLADES = 3

core_square = 0.05
time_step = 0.05

LANES = 128
FEATURES = 32
UNROLL = 16
BF = jnp.bfloat16
F32 = jnp.float32

SMEM = pl.BlockSpec(memory_space=pltpu.SMEM)
VMEM = pl.BlockSpec(memory_space=pltpu.VMEM)


def params(limit=48 << 20):
    return pltpu.CompilerParams(vmem_limit_bytes=limit)


def split3(value):
    high = value.astype(BF).astype(F32)
    rest = value - high
    middle = rest.astype(BF).astype(F32)
    return high, middle, rest - middle


def meta_kernel(blocks, boxes, rcap, cap, move, age, fetch, meta, move_place, age_place, fill):
    def clear(p, carry):
        for lane in range(rcap):
            meta[p, lane] = fetch[p, lane]
        for lane in range(2 * cap):
            meta[p, rcap + lane] = -1
        fill[p] = 0
        fill[boxes + p] = 0
        return carry

    lax.fori_loop(0, boxes, clear, 0)

    def place(g, carry):
        for source, first, target, lane in (
            (move, 0, move_place, rcap),
            (age, boxes, age_place, rcap + cap),
        ):
            block = source[g]
            box = lax.div(block, blocks)
            rank = fill[first + box]
            fill[first + box] = rank + 1
            meta[box, lane + rank] = block - box * blocks
            target[g] = box * 256 + rank
        return carry

    lax.fori_loop(0, blocks, place, 0)


def history_kernel(blocks, cap, place, history, packed):
    def one(g, carry):
        where = place[g]
        box = where >> 8
        rank = where & 255
        packed[box, pl.ds(rank, 3, stride=cap), :] = history[g, 0]
        packed[box, pl.ds(3 * cap + rank, 3, stride=cap), :] = history[g, 1]
        return carry

    lax.fori_loop(0, blocks, one, 0, unroll=4)


def list_kernel(blocks, kmax, slots, limit, tiles, slot_list, pair_list, used, totals,
                ranked, counted, ranked_s, counted_s, sems):
    groups = slots // LANES
    lane = lax.broadcasted_iota(jnp.int32, (blocks, LANES), 1)
    row = lax.broadcasted_iota(jnp.int32, (blocks, LANES), 0)
    before = (
        lax.broadcasted_iota(jnp.int32, (blocks, blocks), 1)
        < lax.broadcasted_iota(jnp.int32, (blocks, blocks), 0)
    ).astype(BF)
    for group in range(groups):
        count = jnp.zeros((blocks, LANES), jnp.int32)
        for k in range(kmax):
            count = count + jnp.where(tiles[:, k : k + 1] == lane + group * LANES, 1, 0)
        present = (count > 0).astype(F32)
        rank = jnp.dot(before, present.astype(BF), preferred_element_type=F32).astype(jnp.int32)
        rank = jnp.where(count > 0, rank, -1)
        entry = row + count * 256
        number = jnp.sum(present, axis=0, keepdims=True).astype(jnp.int32)
        counted[group * 8 : (group + 1) * 8, :] = jnp.broadcast_to(number, (8, LANES))

        def fill(r, carry):
            found = jnp.sum(jnp.where(rank == r, entry, 0), axis=0, keepdims=True)
            ranked[pl.ds(group * blocks + r, 1), :] = found
            return carry

        lax.fori_loop(0, ((jnp.max(number) + 1) >> 1) << 1, fill, 0)
    copies = [
        pltpu.make_async_copy(ranked, ranked_s, sems.at[0]),
        pltpu.make_async_copy(counted, counted_s, sems.at[1]),
    ]
    for copy in copies:
        copy.start()
    for copy in copies:
        copy.wait()

    carry = (0, 0)
    for group in range(groups):

        def flatten(col, carry):
            filled, users = carry
            half = (counted_s[group * 8, col] + 1) >> 1
            slot = group * LANES + col
            used[users] = slot

            def pair(t, carry):
                first = ranked_s[group * blocks + 2 * t, col]
                second = ranked_s[group * blocks + 2 * t + 1, col]
                slot_list[filled + t] = slot
                pair_list[filled + t] = first + second * 65536
                return carry

            lax.fori_loop(0, half, pair, 0)
            return filled + half, users + jnp.where(half > 0, 1, 0)

        carry = lax.fori_loop(0, LANES, flatten, carry)
    filled, users = carry
    for t in range(UNROLL):
        slot_list[filled + t] = used[0]
        pair_list[filled + t] = 0
    for t in range(8):
        used[users + t] = used[0]
    totals[0] = lax.div(filled + (UNROLL - 1), UNROLL)
    totals[1] = (users + 7) >> 3


def target_kernel(blocks, positions, blade, hub, azimuth, feats, centre, tables, stage):
    total = jnp.zeros((3, LANES), F32)
    for b in range(blocks):
        total = total + positions[b]
    middle = jnp.sum(total, axis=1, keepdims=True) / (blocks * LANES)
    middle = jnp.broadcast_to(middle, (3, LANES))
    centre[0:3, :] = middle
    ones = jnp.ones((8, LANES), F32)
    pad = jnp.zeros((FEATURES - 24, LANES), F32)
    for group in range(blocks // 8):
        at = [
            positions[group * 8 : group * 8 + 8, axis, :] - middle[axis : axis + 1, :]
            for axis in range(3)
        ]
        norm = split3(at[0] * at[0] + at[1] * at[1] + at[2] * at[2] + core_square)
        parts = [split3(-2.0 * value) for value in at]
        rows = []
        for piece in (0, 1, 2, 0, 1, 0):
            rows += [parts[axis][piece] for axis in range(3)]
        rows += [ones, ones, ones, norm[0], norm[1], norm[2]]
        base = (group % 2) * 24 * 8
        for f, value in enumerate(rows):
            stage[base + f * 8 : base + f * 8 + 8, :] = value
        for t in range(8):
            picked = stage[pl.ds(base + t, 24, stride=8), :]
            feats[group * 8 + t] = jnp.concatenate([picked, pad], axis=0).astype(BF)
    lane = lax.broadcasted_iota(jnp.int32, (8, LANES), 1)
    angle = jnp.zeros((8, LANES), F32)
    hubs = [jnp.zeros((8, LANES), F32) for _ in range(3)]
    for q in range(ROTORS * BLADES):
        turn = F32(2.0 * math.pi) * F32(q % BLADES) / F32(BLADES)
        angle = jnp.where(lane == q, azimuth[q // BLADES] + turn, angle)
        for axis in range(3):
            hubs[axis] = jnp.where(lane == q, hub[q // BLADES, axis], hubs[axis])
    sources = [jnp.cos(angle), jnp.sin(angle)] + hubs
    for group in range(blocks // 8):
        index = blade[group * 8 : group * 8 + 8, :]
        for n, source in enumerate(sources):
            tables[n, group * 8 : group * 8 + 8, :] = jnp.take_along_axis(source, index, axis=1)


def answer_kernel(boxes, rcap, asked, positions, strengths, packed):
    def one(p, carry):
        for i in range(rcap):
            block = jnp.maximum(asked[p, i], 0)
            packed[p, pl.ds(i, 3, stride=rcap), :] = positions[block]
            packed[p, pl.ds(3 * rcap + i, 3, stride=rcap), :] = strengths[block]
        return carry

    lax.fori_loop(0, boxes, one, 0)


def arrival_kernel(boxes, rcap, cap, blocks, labels, moved_from, aged_from):
    def one(p, carry):
        for rank in range(cap):
            for target, lane in ((moved_from, rcap), (aged_from, rcap + cap)):
                label = labels[p, lane + rank]
                target[jnp.where(label < 0, blocks, label)] = p * 256 + rank
        return carry

    lax.fori_loop(0, boxes, one, 0)


def velocity_kernel(blocks, boxes, rcap, cap, slot_list, pair_list, used, totals, moved_from,
                    age_place, fetched, arrived, positions, targets, centre,
                    new_positions, new_history, outgoing,
                    stage, table_stage, feats, tables, sums, speed):
    rows = 24 * 8
    ones = jnp.ones((8, LANES), F32)
    zeros = jnp.zeros((8, LANES), F32)

    def prepare(o, carry):
        at = [
            fetched[o, axis * rcap : (axis + 1) * rcap, :] - centre[axis : axis + 1, :]
            for axis in range(3)
        ]
        gamma = [fetched[o, (3 + axis) * rcap : (4 + axis) * rcap, :] for axis in range(3)]
        parts = [split3(value) for value in at]
        norm = split3(at[0] * at[0] + at[1] * at[1] + at[2] * at[2])
        values = []
        for piece in (0, 0, 0, 1, 1, 2):
            values += [parts[axis][piece] for axis in range(3)]
        values += [norm[0], norm[1], norm[2], ones, ones, ones]
        for f, value in enumerate(values):
            stage[o, f * 8 : f * 8 + 8, :] = value
        for axis in range(3):
            left, right = (axis + 1) % 3, (axis + 2) % 3
            table_stage[o, axis * 8 : axis * 8 + 8, :] = gamma[axis]
            table_stage[o, (3 + axis) * 8 : (4 + axis) * 8, :] = (
                at[left] * gamma[right] - at[right] * gamma[left]
            )
        table_stage[o, 48:56, :] = zeros
        table_stage[o, 56:64, :] = zeros
        return carry

    lax.fori_loop(0, boxes, prepare, 0)
    identity = (
        lax.broadcasted_iota(jnp.int32, (LANES, LANES), 0)
        == lax.broadcasted_iota(jnp.int32, (LANES, LANES), 1)
    ).astype(BF)
    pad = jnp.zeros((FEATURES - 24, LANES), F32)

    def build(it, carry):
        for u in range(8):
            slot = used[it * 8 + u]
            o = slot >> 3
            i = slot & 7
            picked = jnp.concatenate([stage[o, pl.ds(i, 24, stride=8), :], pad], axis=0)
            turned = lax.dot_general(
                identity, picked.astype(BF), (((1,), (1,)), ((), ())), preferred_element_type=F32
            )
            feats[slot] = turned.astype(BF)
            table = table_stage[o, pl.ds(i, 8, stride=8), :]
            high = table.astype(BF).astype(F32)
            left = jnp.concatenate([high, table - high], axis=0)
            right = jnp.concatenate([high, zeros], axis=0)
            tables[slot] = jnp.concatenate([left, right], axis=1).astype(BF)
        return carry

    lax.fori_loop(0, totals[1], build, 0)
    sums[...] = jnp.zeros_like(sums)

    def accumulate(it, carry):
        found = []
        for u in range(UNROLL):
            slot = slot_list[it * UNROLL + u]
            pair = pair_list[it * UNROLL + u]
            first = pair & 255
            second = (pair >> 16) & 255
            both = jnp.concatenate([targets[first], targets[second]], axis=1)
            inverse = lax.rsqrt(jnp.dot(feats[slot], both, preferred_element_type=F32))
            weight = inverse * inverse * inverse
            high = weight.astype(BF)
            low = (weight - high.astype(F32)).astype(BF)
            summed = jnp.dot(
                tables[slot], jnp.concatenate([high, low], axis=0), preferred_element_type=F32
            )
            times = (((pair >> 8) & 255).astype(F32), (pair >> 24).astype(F32))
            found.append((first, second, times, summed))
        for first, second, times, summed in found:
            for target, factor, part in (
                (first, times[0], summed[:, :LANES]),
                (second, times[1], summed[:, LANES:]),
            ):
                at = pl.ds(pl.multiple_of(target * 16, 16), 16)
                sums[at, :] = sums[at, :] + factor * part
        return carry

    lax.fori_loop(0, totals[0], accumulate, 0)

    scale = 1.0 / (4.0 * math.pi)
    for group in range(blocks // 8):
        first = group * 8
        total = [
            sums[pl.ds(first * 16 + f, 8, stride=16), :]
            + sums[pl.ds(first * 16 + 8 + f, 8, stride=16), :]
            for f in range(6)
        ]
        at = [positions[first : first + 8, axis, :] - centre[axis : axis + 1, :] for axis in range(3)]
        for axis in range(3):
            left, right = (axis + 1) % 3, (axis + 2) % 3
            speed[axis * blocks + first : axis * blocks + first + 8, :] = scale * (
                at[left] * total[right] - at[right] * total[left] - total[3 + axis]
            )
    unused = jnp.zeros((3 * cap, LANES), F32)

    def clear(p, carry):
        outgoing[p] = unused
        return carry

    lax.fori_loop(0, boxes, clear, 0)

    def finish(b, carry):
        where = moved_from[b]
        box = where >> 8
        rank = where & 255
        recent = arrived[box, pl.ds(rank, 3, stride=cap), :]
        older = arrived[box, pl.ds(3 * cap + rank, 3, stride=cap), :]
        now = speed[pl.ds(b, 3, stride=blocks), :]
        stepped = positions[b] + time_step * (23.0 * now - 16.0 * recent + 5.0 * older) / 12.0
        new_positions[b] = stepped
        new_history[b, 0] = now
        new_history[b, 1] = recent
        out = age_place[b]
        outgoing[out >> 8, pl.ds(out & 255, 3, stride=cap), :] = stepped
        return carry

    lax.fori_loop(0, blocks, finish, 0, unroll=4)


def frame_kernel(blocks, cap, aged_from, arrived, tables, frame):
    def one(b, carry):
        where = aged_from[b]
        aged = arrived[where >> 8, pl.ds(where & 255, 3, stride=cap), :]
        cosine, sine, hub0, hub1, hub2 = [tables[n, pl.ds(b, 1), :] for n in range(5)]
        first = aged[0:1] - hub0
        second = aged[1:2] - hub1
        frame[b, 0:1, :] = cosine * first + sine * second
        frame[b, 1:2, :] = cosine * second - sine * first
        frame[b, 2:3, :] = aged[2:3] - hub2
        return carry

    lax.fori_loop(0, blocks, one, 0, unroll=8)


def swap(values):
    return lax.all_to_all(values, "box", split_axis=0, concat_axis=0, tiled=True)


def body(
    positions,
    strengths,
    history,
    move_list,
    age_slot,
    fetch_list,
    tile_slot,
    tile_count,
    blade_id,
    hub_centre,
    azimuth,
):
    blocks = positions.shape[0]
    boxes = lax.axis_size("box")
    rcap = fetch_list.shape[2]
    kmax = tile_slot.shape[1]
    cap = 2 * blocks // boxes
    slots = boxes * rcap
    limit = (blocks * kmax + slots) // 2 + 2 * UNROLL

    def shape(dims, dtype=F32):
        return jax.ShapeDtypeStruct(dims, dtype)

    meta, move_place, age_place = pl.pallas_call(
        functools.partial(meta_kernel, blocks, boxes, rcap, cap),
        in_specs=[SMEM] * 3,
        out_specs=[SMEM] * 3,
        out_shape=[
            shape((boxes, LANES), jnp.int32),
            shape((blocks,), jnp.int32),
            shape((blocks,), jnp.int32),
        ],
        scratch_shapes=[pltpu.SMEM((2 * boxes,), jnp.int32)],
        name="meta",
    )(move_list, age_slot, fetch_list[0])
    labels = swap(meta)
    packed_history = pl.pallas_call(
        functools.partial(history_kernel, blocks, cap),
        in_specs=[SMEM, VMEM],
        out_specs=VMEM,
        out_shape=shape((boxes, 6 * cap, LANES)),
        name="pack_history",
    )(move_place, history)
    tiles = jnp.where(
        jnp.arange(kmax, dtype=jnp.int32)[None, :] < tile_count[:, None], tile_slot, -1
    )
    groups = slots // LANES
    slot_list, pair_list, used, totals = pl.pallas_call(
        functools.partial(list_kernel, blocks, kmax, slots, limit),
        in_specs=[VMEM],
        out_specs=[SMEM] * 4,
        out_shape=[
            shape((limit,), jnp.int32),
            shape((limit,), jnp.int32),
            shape((slots + 8,), jnp.int32),
            shape((2,), jnp.int32),
        ],
        scratch_shapes=[
            pltpu.VMEM((groups * blocks, LANES), jnp.int32),
            pltpu.VMEM((groups * 8, LANES), jnp.int32),
            pltpu.SMEM((groups * blocks, LANES), jnp.int32),
            pltpu.SMEM((groups * 8, LANES), jnp.int32),
            pltpu.SemaphoreType.DMA((2,)),
        ],
        name="pair_list",
    )(tiles)
    targets, centre, tables = pl.pallas_call(
        functools.partial(target_kernel, blocks),
        in_specs=[VMEM, VMEM, SMEM, SMEM],
        out_specs=[VMEM] * 3,
        out_shape=[
            shape((blocks, FEATURES, LANES), BF),
            shape((8, LANES)),
            shape((5, blocks, LANES)),
        ],
        scratch_shapes=[pltpu.VMEM((2 * 24 * 8, LANES), F32)],
        name="target_features",
    )(positions, blade_id, hub_centre, azimuth)
    answers = pl.pallas_call(
        functools.partial(answer_kernel, boxes, rcap),
        in_specs=[SMEM, VMEM, VMEM],
        out_specs=VMEM,
        out_shape=shape((boxes, 6 * rcap, LANES)),
        name="answer",
    )(labels, positions, strengths)
    fetched = swap(answers)
    arrived = swap(packed_history)
    moved_from, aged_from = pl.pallas_call(
        functools.partial(arrival_kernel, boxes, rcap, cap, blocks),
        in_specs=[SMEM],
        out_specs=[SMEM] * 2,
        out_shape=[shape((blocks + 1,), jnp.int32)] * 2,
        name="arrivals",
    )(labels)
    new_positions, new_history, outgoing = pl.pallas_call(
        functools.partial(velocity_kernel, blocks, boxes, rcap, cap),
        in_specs=[SMEM] * 6 + [VMEM] * 5,
        out_specs=[VMEM] * 3,
        out_shape=[
            shape((blocks, 3, LANES)),
            shape((blocks, 2, 3, LANES)),
            shape((boxes, 3 * cap, LANES)),
        ],
        scratch_shapes=[
            pltpu.VMEM((boxes, 24 * 8, LANES), F32),
            pltpu.VMEM((boxes, 64, LANES), F32),
            pltpu.VMEM((slots, LANES, FEATURES), BF),
            pltpu.VMEM((slots, 16, 2 * LANES), BF),
            pltpu.VMEM((blocks * 16, LANES), F32),
            pltpu.VMEM((3 * blocks, LANES), F32),
        ],
        compiler_params=params(),
        name="velocity",
    )(
        slot_list, pair_list, used, totals, moved_from, age_place,
        fetched, arrived, positions, targets, centre,
    )
    aged = swap(outgoing)
    frame = pl.pallas_call(
        functools.partial(frame_kernel, blocks, cap),
        in_specs=[SMEM, VMEM, VMEM],
        out_specs=VMEM,
        out_shape=shape((blocks, 3, LANES)),
        name="frame",
    )(aged_from, aged, tables)
    return new_positions, new_history, frame


def solution(mesh):
    split = ("cases", "box")
    placed = (
        P(split, None, None),
        P(split, None, None),
        P(split, None, None, None),
        P(split),
        P(split),
        P(split, None, None),
        P(split, None),
        P(split),
        P(split, None),
        P("cases", None),
        P("cases"),
    )
    return jax.shard_map(
        body,
        mesh=mesh,
        in_specs=placed,
        out_specs=(P(split, None, None), P(split, None, None, None), P(split, None, None)),
        check_vma=False,
    )
```

time: 344 us -> 106 us (0.31)
  matrix products: 192 us -> 0 us
  local copies, waits for them, and re-layouts: 70.9 us -> 12 us
  Pallas kernels: 0 us -> 50.3 us
  between operations: 14.4 us -> 0.8 us
  other arithmetic: 12.3 us -> 0.69 us
  waiting for transfers between devices: 25.5 us -> 18.7 us
  starting transfers between devices: 25.7 us -> 21.5 us
    dot_general x16 -> x0, matrix products: 192 us -> none  [induced(): jnp.einsum('kij,kcj->ci', weight, source_table, precision=lax.Precision.H...]
    pallas_call x0 -> x8, Pallas kernels: none -> 50.3 us  [the longest x1 26.6 us: body(): pl.pallas_call(functools.partial(velocity_kernel, blocks, boxes, rcap, ca...]
    gather x33 -> x0, local copies, waits for them, and re-layouts: 27 us -> none  [the longest x16 12.2 us: one_target(): jnp.take(source_table, slots, axis=0)]
    scatter x6 -> x0, local copies, waits for them, and re-layouts: 25.3 us -> none  [the longest x2 14.5 us: pack_blocks(): jnp.zeros((box_count * capacity,) + values.shape[1:], values.dtype)]
    unnamed x10 -> x40, local copies, waits for them, and re-layouts: 2.31 us -> 10.6 us
    all_to_all x4, waiting for transfers between devices: 25.5 us -> 18.7 us  [swap(): lax.all_to_all(values, 'box', split_axis=0, concat_axis=0, tiled=True)]
    all_gather x1 -> x0, local copies, waits for them, and re-layouts: 5.7 us -> none  [body(): everything = lax.all_gather(offered, 'box', axis=0, tiled=True)]
    all_to_all x4, starting transfers between devices: 25.6 us -> 21.5 us  [swap(): lax.all_to_all(values, 'box', split_axis=0, concat_axis=0, tiled=True)]
  transfers between devices with their start and end apart: 5 -> 4, of which waited for: 2 -> 3; matrix products, arithmetic and copies ran while one was open for 78% -> 6% of each run, Pallas kernels for 0% -> 18%
where the time goes in v1:
time: 106 us; the launch traced here: 104 us
  Pallas kernels  50.3 us (47%)
  starting transfers between devices  21.5 us (20%)
  waiting for transfers between devices  18.7 us (18%)
  local copies, waits for them, and re-layouts  12 us (11%)
    pallas_call x1, Pallas kernels, body(): pl.pallas_call(functools.partial(velocity_kernel, blocks, boxes, rcap, ca...  26.6 us
    all_to_all x4, starting transfers between devices, swap(): lax.all_to_all(values, 'box', split_axis=0, concat_axis=0, tiled=True)  21.5 us
    all_to_all x4, waiting for transfers between devices, swap(): lax.all_to_all(values, 'box', split_axis=0, concat_axis=0, tiled=True)  18.7 us
    unnamed x40, local copies, waits for them, and re-layouts  10.6 us
    pallas_call x1, Pallas kernels, body(): pl.pallas_call(functools.partial(list_kernel, blocks, kmax, slots, limit)...  10.2 us
    pallas_call x1, Pallas kernels, body(): pl.pallas_call(functools.partial(meta_kernel, blocks, boxes, rcap, cap),...  3.22 us
    pallas_call x1, Pallas kernels, body(): pl.pallas_call(functools.partial(target_kernel, blocks), in_specs=[VMEM,...  2.54 us
  transfers between devices with their start and end apart: 4, of which 3 were waited for; matrix products, arithmetic and copies ran while one was open for 6% of the time, Pallas kernels for 18%

profile of v1, /device:TPU:0, one launch (start us, length us, event | category | flops | bytes accessed | tf_op | source)
XLA Modules:
  0.0 104.1 jit_solution(12704886884662357100)
XLA Ops:
  0.6 1.4 %copy.26.fetch = s32[16,8]{1,0:T(8,128)} copy(s32[16,8]{0,1:T(8,128)} %bitcast.8) | data formatting | bytes 1024 | tf_op jit(solution)/shard_map/squeeze | solution.py:387
  2.0 3.2 %meta.1 = (s32[16,128]{1,0:T(8,128)}, s32[64]{0:T(128)}, s32[64]{0:T(128)}) custom-call(s32[64]{0:T(128)} %move.1, s32[64]{0:T(128)} %age.1, s32[16,8]{1,0:T(8,128)} %copy.26.fetch), custom_call_target="tpu_custom_call" | custom-call | tf_op jit(solution)/shard_map/meta/pallas_call | solution.py:376
  5.2 7.4 %all-to-all-start = ((s32[16,1,128]{2,1,0:T(1,128)}), s32[16,1,128]{2,1,0:T(1,128)S(1)}, u32[]{:S(2)}, u32[]{:S(2)}) async-start(s32[16,1,128]{2,1,0:T(1,128)} %bitcast.7), calls=%async_computation | async-start | bytes 16384 | tf_op jit(solution)/shard_map/all_to_all | solution.py:349
  12.6 1.7 %copy.30.history = f32[64,2,3,128]{3,2,1,0:T(4,128)} copy(f32[64,2,3,128]{3,1,2,0:T(2,128)} %param.13) | data formatting | bytes 393216 | tf_op args[2]
  14.3 1.9 %pack_history.1 = f32[16,48,128]{2,1,0:T(8,128)} custom-call(s32[64]{0:T(128)} %get-tuple-element.25.place, f32[64,2,3,128]{3,2,1,0:T(4,128)} %copy.30.history), custom_call_target="tpu_custom_call" | custom-call | tf_op jit(solution)/shard_map/pack_history/pallas_call | solution.py:389
  16.2 2.7 %all-to-all-done = s32[16,1,128]{2,1,0:T(1,128)S(1)} async-done(((s32[16,1,128]{2,1,0:T(1,128)}), s32[16,1,128]{2,1,0:T(1,128)S(1)}, u32[]{:S(2)}, u32[]{:S(2)}) %all-to-all-start) | async-done | bytes 8224 | tf_op jit(solution)/shard_map/all_to_all | solution.py:349
  18.9 0.6 copy-done.12
  19.5 3.6 %all-to-all-start.2 = ((f32[16,48,128]{2,1,0:T(8,128)}), f32[16,48,128]{2,1,0:T(8,128)S(1)}, u32[]{:S(2)}, u32[]{:S(2)}) async-start(f32[16,48,128]{2,1,0:T(8,128)} %pack_history.1), calls=%async_computation.2 | async-start | bytes 786432 | tf_op jit(solution)/shard_map/all_to_all | solution.py:349
  23.1 0.7 copy.28.positions
  23.8 0.2 copy-done.11
  24.0 0.7 copy.29.strengths
  24.7 2.1 %answer.1 = f32[16,48,128]{2,1,0:T(8,128)} custom-call(s32[16,128]{1,0:T(8,128)} %bitcast.5, f32[64,3,128]{2,1,0:T(4,128)} %copy.28.positions, f32[64,3,128]{2,1,0:T(4,128)} %copy.29.strengths), custom_call_target="tpu_custom_call" | custom-call | tf_op jit(solution)/shard_map/answer/pallas_call | solution.py:431
  26.8 8.4 %all-to-all-done.2.arrived = f32[16,48,128]{2,1,0:T(8,128)S(1)} async-done(((f32[16,48,128]{2,1,0:T(8,128)}), f32[16,48,128]{2,1,0:T(8,128)S(1)}, u32[]{:S(2)}, u32[]{:S(2)}) %all-to-all-start.2) | async-done | bytes 393248 | tf_op jit(solution)/shard_map/all_to_all | solution.py:349
  35.3 3.7 %all-to-all-start.1 = ((f32[16,48,128]{2,1,0:T(8,128)}), f32[16,48,128]{2,1,0:T(8,128)S(1)}, u32[]{:S(2)}, u32[]{:S(2)}) async-start(f32[16,48,128]{2,1,0:T(8,128)} %answer.1), calls=%async_computation.1 | async-start | bytes 786432 | tf_op jit(solution)/shard_map/all_to_all | solution.py:349
  39.0 0.7 copy.32.hub
  39.6 0.1 copy.25
  39.7 0.6 copy-done.15
  40.3 0.7 fusion.tiles
  41.0 10.2 %pair_list.1 = (s32[1120]{0:T(1024)}, s32[1120]{0:T(1024)}, s32[136]{0:T(256)}, s32[2]{0:T(128)}) custom-call(s32[64,32]{1,0:T(8,128)} %fusion.tiles), custom_call_target="tpu_custom_call" | custom-call | tf_op jit(solution)/shard_map/pair_list/pallas_call | solution.py:400
  51.2 2.5 %target_features.1 = (bf16[64,32,128]{2,1,0:T(8,128)(2,1)}, f32[8,128]{1,0:T(8,128)}, f32[5,64,128]{2,1,0:T(8,128)}) custom-call(f32[64,3,128]{2,1,0:T(4,128)} %copy.28.positions, s32[64,128]{1,0:T(8,128)} %blade.1, f32[6,3]{1,0:T(8,128)} %copy.32.hub, f32[6]{0:T(128)} %azimuth.1), custom_call_target="tpu_custom_call" | custom-call | tf_op jit(solution)/shard_map/target_features/pallas_call | solution.py:419
  53.7 1.9 %arrivals.1 = (s32[65]{0:T(128)}, s32[65]{0:T(128)}) custom-call(s32[16,128]{1,0:T(8,128)} %bitcast.6), custom_call_target="tpu_custom_call" | custom-call | tf_op jit(solution)/shard_map/arrivals/pallas_call | solution.py:440
  55.7 0.6 copy-done.2
  56.3 0.0 copy-done.4
  56.4 1.0 copy-done.1
  57.4 26.6 %velocity.1 = (f32[64,3,128]{2,1,0:T(4,128)S(1)}, f32[64,2,3,128]{3,2,1,0:T(4,128)S(1)}, f32[16,24,128]{2,1,0:T(8,128)}) custom-call(s32[1120]{0:T(1024)S(1)} %copy-done.2, s32[1120]{0:T(1024)S(1)} %copy-done.3, s32[136]{0:T(256)S(1)} %copy-done.5, s32[2]{0:T(128)S(1)} %copy-done.7, s32[65]{0:T(128)S(1)} %copy-done.8, s32[64]{0:T(128)S(1)} %copy-done.6, ...), custom_call_target="tpu_custom_call" | custom-call | tf_op jit(solution)/shard_map/velocity/pallas_call | solution.py:447
  84.1 6.9 %all-to-all-start.3 = ((f32[16,24,128]{2,1,0:T(8,128)}), f32[16,24,128]{2,1,0:T(8,128)S(1)}, u32[]{:S(2)}, u32[]{:S(2)}) async-start(f32[16,24,128]{2,1,0:T(8,128)} %get-tuple-element.31), calls=%async_computation.3 | async-start | bytes 393216 | tf_op jit(solution)/shard_map/all_to_all | solution.py:349
  90.9 0.6 copy.34
  91.6 0.8 copy.35
  92.4 7.6 %all-to-all-done.3.arrived = f32[16,24,128]{2,1,0:T(8,128)S(1)} async-done(((f32[16,24,128]{2,1,0:T(8,128)}), f32[16,24,128]{2,1,0:T(8,128)S(1)}, u32[]{:S(2)}, u32[]{:S(2)}) %all-to-all-start.3) | async-done | bytes 196640 | tf_op jit(solution)/shard_map/all_to_all | solution.py:349
  99.9 0.7 copy-done.9
  100.6 1.9 %frame.1 = f32[64,3,128]{2,1,0:T(4,128)} custom-call(s32[65]{0:T(128)} %get-tuple-element.30.aged_from, f32[16,24,128]{2,1,0:T(8,128)} %copy-done.9, f32[5,64,128]{2,1,0:T(8,128)} %get-tuple-element.32.tables), custom_call_target="tpu_custom_call" | custom-call | tf_op jit(solution)/shard_map/frame/pallas_call | solution.py:471
  102.5 1.6 %copy.36 = f32[64,3,128]{2,0,1:T(8,128)} copy(f32[64,3,128]{2,1,0:T(4,128)} %frame.1) | data formatting | bytes 196608
  (26 shorter events, 0.1 us)
Async XLA Ops:
  5.2 13.7 %all-to-all-start = ((s32[16,1,128]{2,1,0:T(1,128)}), s32[16,1,128]{2,1,0:T(1,128)S(1)}, u32[]{:S(2)}, u32[]{:S(2)}) async-start(s32[16,1,128]{2,1,0:T(1,128)} %bitcast.7), calls=%async_computation | async-start | bytes 16384 | tf_op jit(solution)/shard_map/all_to_all | solution.py:349
  16.2 6.9 %copy-start.10 = (f32[64,3,128]{2,0,1:T(8,128)S(1)}, f32[64,3,128]{2,0,1:T(8,128)}, u32[]{:S(2)}) copy-start(f32[64,3,128]{2,0,1:T(8,128)} %param.11) | copy-start | bytes 294916
  18.9 0.6 copy-start.12
  19.5 15.7 %all-to-all-start.2 = ((f32[16,48,128]{2,1,0:T(8,128)}), f32[16,48,128]{2,1,0:T(8,128)S(1)}, u32[]{:S(2)}, u32[]{:S(2)}) async-start(f32[16,48,128]{2,1,0:T(8,128)} %pack_history.1), calls=%async_computation.2 | async-start | bytes 786432 | tf_op jit(solution)/shard_map/all_to_all | solution.py:349
  23.1 0.9 copy-start.11
  26.8 12.1 %copy-start.14 = (f32[6,3]{0,1:T(4,128)S(1)}, f32[6,3]{0,1:T(4,128)}, u32[]{:S(2)}) copy-start(f32[6,3]{0,1:T(4,128)} %param.20) | copy-start | bytes 220
  35.3 4.4 %copy-start.13 = (s32[64,32]{0,1:T(8,128)S(1)}, s32[64,32]{0,1:T(8,128)}, u32[]{:S(2)}) copy-start(s32[64,32]{0,1:T(8,128)} %param.17) | copy-start | bytes 24580
  35.3 20.4 %all-to-all-start.1 = ((f32[16,48,128]{2,1,0:T(8,128)}), f32[16,48,128]{2,1,0:T(8,128)S(1)}, u32[]{:S(2)}, u32[]{:S(2)}) async-start(f32[16,48,128]{2,1,0:T(8,128)} %answer.1), calls=%async_computation.1 | async-start | bytes 786432 | tf_op jit(solution)/shard_map/all_to_all | solution.py:349
  39.6 0.7 copy-start.15
  40.3 15.4 %copy-start = (f32[64,3,128]{2,1,0:T(4,128)S(1)}, f32[64,3,128]{2,1,0:T(4,128)}, u32[]{:S(2)}) copy-start(f32[64,3,128]{2,1,0:T(4,128)} %copy.28.positions) | copy-start | bytes 294916
  53.7 2.0 %copy-start.3 = (s32[1120]{0:T(1024)S(1)}, s32[1120]{0:T(1024)}, u32[]{:S(2)}) copy-start(s32[1120]{0:T(1024)} %get-tuple-element.19.pair_list) | copy-start | bytes 13444
  55.6 0.7 copy-start.2
  55.7 0.7 copy-start.4
  55.7 0.7 copy-start.7
  55.7 0.7 copy-start.8
  55.7 0.7 copy-start.5
  55.7 0.7 copy-start.6
  56.4 1.0 %copy-start.1 = (bf16[64,32,128]{2,1,0:T(8,128)(2,1)S(1)}, bf16[64,32,128]{2,1,0:T(8,128)(2,1)}, u32[]{:S(2)}) copy-start(bf16[64,32,128]{2,1,0:T(8,128)(2,1)} %get-tuple-element.26.targets) | copy-start | bytes 1572868
  84.1 15.9 %all-to-all-start.3 = ((f32[16,24,128]{2,1,0:T(8,128)}), f32[16,24,128]{2,1,0:T(8,128)S(1)}, u32[]{:S(2)}, u32[]{:S(2)}) async-start(f32[16,24,128]{2,1,0:T(8,128)} %get-tuple-element.31), calls=%async_computation.3 | async-start | bytes 393216 | tf_op jit(solution)/shard_map/all_to_all | solution.py:349
  99.9 0.7 copy-start.9

commit v2 on v1

v2 whole, which is shorter than its diff:
```python
import functools
import math

import jax
import jax.numpy as jnp
from jax import lax
from jax.experimental import pallas as pl
from jax.experimental.pallas import tpu as pltpu
from jax.sharding import PartitionSpec as P

ROTORS = 6
BLADES = 3

core_square = 0.05
time_step = 0.05

LANES = 128
UNROLL = 32
BUILD = 8
BF = jnp.bfloat16
F32 = jnp.float32
I32 = jnp.int32

SMEM = pl.BlockSpec(memory_space=pltpu.SMEM)
VMEM = pl.BlockSpec(memory_space=pltpu.VMEM)


def split3(value):
    high = value.astype(BF).astype(F32)
    rest = value - high
    middle = rest.astype(BF).astype(F32)
    return high, middle, rest - middle


def iota(dims, axis):
    return lax.broadcasted_iota(I32, dims, axis)


def meta_kernel(blocks, boxes, rcap, cap, move, age, fetch, meta, move_place, age_place, fill):
    def ask(p, carry):
        for lane in range(rcap):
            meta[p, lane] = fetch[lane, p]
        fill[p] = 0
        fill[boxes + p] = 0
        return carry

    lax.fori_loop(0, boxes, ask, 0, unroll=4)

    def place(g, carry):
        for source, first, target, lane in (
            (move, 0, move_place, rcap),
            (age, boxes, age_place, rcap + cap),
        ):
            block = source[g]
            box = lax.div(block, blocks)
            rank = fill[first + box]
            fill[first + box] = rank + 1
            meta[box, lane + rank] = block - box * blocks
            target[g] = box * 256 + rank
        return carry

    lax.fori_loop(0, blocks, place, 0, unroll=4)

    def number(p, carry):
        meta[p, rcap + 2 * cap] = fill[p]
        meta[p, rcap + 2 * cap + 1] = fill[boxes + p]
        return carry

    lax.fori_loop(0, boxes, number, 0, unroll=4)


def history_kernel(blocks, boxes, rcap, cap, place, labels, history, packed, moved_from, aged_from):
    def one(g, carry):
        where = place[g]
        box = where >> 8
        rank = where & 255
        for axis in range(3):
            packed[box, pl.ds(axis * cap + rank, 2, stride=3 * cap), :] = history[g, axis]
        return carry

    lax.fori_loop(0, blocks, one, 0, unroll=4)

    def peer(p, carry):
        for target, lane, number in ((moved_from, rcap, 0), (aged_from, rcap + cap, 1)):

            def label(rank, carry):
                target[labels[p, lane + rank]] = p * 256 + rank
                return carry

            lax.fori_loop(0, labels[p, rcap + 2 * cap + number], label, 0)
        return carry

    lax.fori_loop(0, boxes, peer, 0)


def plan_rows(slots, most):
    chunks = (most + LANES - 1) // LANES
    users = (slots + BUILD + LANES - 1) // LANES
    return chunks, users, (chunks + users + 2 + 7) // 8 * 8


def plan_kernel(blocks, kmax, slots, most, tiles, count, plan, ranked):
    half = kmax
    chunks, users, rows = plan_rows(slots, most)
    slot = iota((slots, blocks), 0)
    times = jnp.zeros((slots, blocks), I32)
    for k in range(kmax):
        named = jnp.where(count[...] > k, tiles[k : k + 1, :], -1)
        times = times + jnp.where(slot == named, 1, 0)
    present = jnp.where(times > 0, 1.0, 0.0)
    inner = jnp.where(iota((blocks, blocks), 0) < iota((blocks, blocks), 1), 1.0, 0.0)
    rank = jnp.dot(present.astype(BF), inner.astype(BF), preferred_element_type=F32)
    rank = jnp.where(times > 0, rank, -2.0)
    number = jnp.dot(
        present.astype(BF), jnp.ones((blocks, LANES), BF), preferred_element_type=F32
    ).astype(I32)
    pairs = (number + 1) >> 1
    outer = jnp.where(iota((slots, slots), 1) <= iota((slots, slots), 0), 1.0, 0.0).astype(BF)
    ends = jnp.dot(outer, pairs.astype(F32).astype(BF), preferred_element_type=F32).astype(I32)
    used = jnp.where(number > 0, 1.0, 0.0).astype(BF)
    tally = jnp.dot(outer, used, preferred_element_type=F32).astype(I32)
    total = ends[slots - 1 : slots, :]
    live = tally[slots - 1 : slots, :]
    opening = jnp.sum(jnp.where(tally <= 0, 1, 0), axis=0, keepdims=True)
    lane = iota((1, LANES), 1)
    for chunk in range(chunks):
        spot = lane + chunk * LANES
        past = ends <= spot
        source = jnp.sum(jnp.where(past, 1, 0), axis=0, keepdims=True)
        start = jnp.max(jnp.where(past, ends, 0), axis=0, keepdims=True)
        word = jnp.where(spot < total, source + (spot - start) * 65536, opening + half * 65536)
        plan[chunk : chunk + 1, :] = word
    for chunk in range(users):
        spot = lane + chunk * LANES
        source = jnp.sum(jnp.where(tally <= spot, 1, 0), axis=0, keepdims=True)
        plan[chunks + chunk : chunks + chunk + 1, :] = jnp.where(spot < live, source, opening)
    plan[rows - 2 : rows - 1, :] = (total + (UNROLL - 1)) >> (UNROLL.bit_length() - 1)
    plan[rows - 1 : rows, :] = (live + (BUILD - 1)) >> (BUILD.bit_length() - 1)
    limit = jnp.max(pairs)
    for group in range(slots // LANES):
        at = slice(group * LANES, (group + 1) * LANES)
        wide = [
            jnp.concatenate([value, jnp.zeros((LANES, LANES - blocks), F32)], axis=1).T[:blocks]
            for value in (rank[at], times[at].astype(F32))
        ]
        position = wide[0].astype(I32)
        entry = iota((blocks, LANES), 0) + wide[1].astype(I32) * 256
        entry = jnp.where((position & 1) == 1, entry * 65536, entry)
        position = position >> 1
        first = group * (half + 8)
        ranked[first + half : first + half + 8, :] = jnp.zeros((8, LANES), I32)

        def fill(t, carry):
            found = jnp.sum(jnp.where(position == t, entry, 0), axis=0, keepdims=True)
            ranked[pl.ds(first + t, 1), :] = found
            return carry

        lax.fori_loop(0, limit, fill, 0)


def target_kernel(blocks, positions, blade, hub, azimuth, feats, centre, tables, stage):
    middle = [
        jnp.sum(positions[axis * blocks : (axis + 1) * blocks, :], axis=(0, 1), keepdims=True)
        / (blocks * LANES)
        for axis in range(3)
    ]
    for axis in range(3):
        centre[axis : axis + 1, :] = jnp.broadcast_to(middle[axis], (1, LANES))
    ones = jnp.ones((8, LANES), F32)
    pad = jnp.zeros((LANES - 24, LANES), F32)
    for group in range(blocks // 8):
        first = group * 8
        at = [
            positions[axis * blocks + first : axis * blocks + first + 8, :] - middle[axis]
            for axis in range(3)
        ]
        norm = split3(at[0] * at[0] + at[1] * at[1] + at[2] * at[2] + core_square)
        parts = [split3(-2.0 * value) for value in at]
        rows = []
        for piece in (0, 1, 2, 0, 1, 0):
            rows += [parts[axis][piece] for axis in range(3)]
        rows += [ones, ones, ones, norm[0], norm[1], norm[2]]
        base = (group % 2) * 24 * 8
        for f, value in enumerate(rows):
            stage[base + f * 8 : base + f * 8 + 8, :] = value
        for t in range(8):
            picked = stage[pl.ds(base + t, 24, stride=8), :]
            feats[first + t] = jnp.concatenate([picked, pad], axis=0).astype(BF)
    lane = iota((8, LANES), 1)
    angle = jnp.zeros((8, LANES), F32)
    hubs = [jnp.zeros((8, LANES), F32) for _ in range(3)]
    for q in range(ROTORS * BLADES):
        turn = F32(2.0 * math.pi) * F32(q % BLADES) / F32(BLADES)
        angle = jnp.where(lane == q, azimuth[q // BLADES] + turn, angle)
        for axis in range(3):
            hubs[axis] = jnp.where(lane == q, hub[axis, q // BLADES], hubs[axis])
    sources = [jnp.cos(angle), jnp.sin(angle)] + hubs
    for group in range(blocks // 8):
        index = blade[group * 8 : group * 8 + 8, :]
        for n, source in enumerate(sources):
            tables[n, group * 8 : group * 8 + 8, :] = jnp.take_along_axis(source, index, axis=1)


def answer_kernel(blocks, boxes, rcap, asked, positions, strengths, packed):
    def one(p, carry):
        for i in range(rcap):
            block = jnp.maximum(asked[p, i], 0)
            packed[p, pl.ds(i, 3, stride=rcap), :] = positions[pl.ds(block, 3, stride=blocks), :]
            packed[p, pl.ds(3 * rcap + i, 3, stride=rcap), :] = strengths[
                pl.ds(block, 3, stride=blocks), :
            ]
        return carry

    lax.fori_loop(0, boxes, one, 0)


def velocity_kernel(blocks, boxes, rcap, slots, half, most, plan, ranked, fetched, positions,
                    targets, centre, speed, stage, table_stage, feats, tables, sums0, sums1, held):
    chunks, _, rows = plan_rows(slots, most)
    ones = jnp.ones((8, LANES), F32)
    zeros = jnp.zeros((8, LANES), F32)

    def prepare(o, carry):
        at = [
            fetched[o, axis * rcap : (axis + 1) * rcap, :] - centre[axis : axis + 1, :]
            for axis in range(3)
        ]
        gamma = [fetched[o, (3 + axis) * rcap : (4 + axis) * rcap, :] for axis in range(3)]
        parts = [split3(value) for value in at]
        norm = split3(at[0] * at[0] + at[1] * at[1] + at[2] * at[2])
        values = []
        for piece in (0, 0, 0, 1, 1, 2):
            values += [parts[axis][piece] for axis in range(3)]
        values += [norm[0], norm[1], norm[2], ones, ones, ones]
        for f, value in enumerate(values):
            stage[o, f * 8 : f * 8 + 8, :] = value
        for axis in range(3):
            left, right = (axis + 1) % 3, (axis + 2) % 3
            table_stage[o, axis * 8 : axis * 8 + 8, :] = gamma[axis]
            table_stage[o, (3 + axis) * 8 : (4 + axis) * 8, :] = (
                at[left] * gamma[right] - at[right] * gamma[left]
            )
        table_stage[o, 48:56, :] = zeros
        table_stage[o, 56:64, :] = zeros
        return carry

    lax.fori_loop(0, boxes, prepare, 0, unroll=2)
    identity = jnp.where(
        iota((LANES, LANES), 0) == iota((LANES, LANES), 1), 1.0, 0.0
    ).astype(BF)
    pad = jnp.zeros((LANES - 24, LANES), F32)

    def build(it, carry):
        for u in range(BUILD):
            at = it * BUILD + u
            slot = plan[chunks + (at >> 7), at & 127]
            o = slot >> 3
            i = slot & 7
            picked = jnp.concatenate([stage[o, pl.ds(i, 24, stride=8), :], pad], axis=0)
            turned = lax.dot_general(
                identity, picked.astype(BF), (((1,), (1,)), ((), ())), preferred_element_type=F32
            )
            feats[slot] = turned.astype(BF)
            table = table_stage[o, pl.ds(i, 8, stride=8), :]
            high = table.astype(BF).astype(F32)
            left = jnp.concatenate([high, table - high], axis=0)
            right = jnp.concatenate([high, zeros], axis=0)
            tables[slot] = jnp.concatenate([left, right], axis=1).astype(BF)
        return carry

    lax.fori_loop(0, plan[rows - 1, 0], build, 0)
    sums0[...] = jnp.zeros_like(sums0)
    sums1[...] = jnp.zeros_like(sums1)
    held[...] = jnp.zeros_like(held)

    def named(it):
        found = []
        for u in range(UNROLL):
            at = it * UNROLL + u
            word = plan[at >> 7, at & 127]
            slot = word & 65535
            row = word >> 16
            if slots > LANES:
                row = row + (slot >> 7) * (half + 8)
            found.append((slot, ranked[row, slot & 127]))
        return found

    def flush(it):
        for u, (_, pair) in enumerate(named(it)):
            for sums, word, part in (
                (sums0, pair & 65535, held[u, :, :LANES]),
                (sums1, pair >> 16, held[u, :, LANES:]),
            ):
                at = pl.ds(pl.multiple_of((word & 255) * 8, 8), 8)
                sums[at, :] = sums[at, :] + (word >> 8).astype(F32) * part

    def accumulate(it, carry):
        flush(jnp.maximum(it - 1, 0))
        for u, (slot, pair) in enumerate(named(it)):
            both = jnp.concatenate([targets[pair & 255], targets[(pair >> 16) & 255]], axis=1)
            inverse = lax.rsqrt(jnp.dot(feats[slot], both, preferred_element_type=F32))
            weight = inverse * inverse * inverse
            high = weight.astype(BF)
            low = (weight - high.astype(F32)).astype(BF)
            summed = jnp.dot(
                tables[slot], jnp.concatenate([high, low], axis=0), preferred_element_type=F32
            )
            held[u] = summed[:8] + summed[8:]
        return carry

    number = plan[rows - 2, 0]
    lax.fori_loop(0, number, accumulate, 0)
    flush(number - 1)

    scale = 1.0 / (4.0 * math.pi)
    for group in range(blocks // 8):
        first = group * 8
        total = [
            sums0[pl.ds(first * 8 + f, 8, stride=8), :] + sums1[pl.ds(first * 8 + f, 8, stride=8), :]
            for f in range(6)
        ]
        at = [
            positions[axis * blocks + first : axis * blocks + first + 8, :]
            - centre[axis : axis + 1, :]
            for axis in range(3)
        ]
        for axis in range(3):
            left, right = (axis + 1) % 3, (axis + 2) % 3
            speed[axis * blocks + first : axis * blocks + first + 8, :] = scale * (
                at[left] * total[right] - at[right] * total[left] - total[3 + axis]
            )


def step_kernel(blocks, boxes, cap, moved_from, age_place, arrived, positions, speed,
                new_positions, new_history, outgoing):
    unused = jnp.zeros((3 * cap, LANES), F32)

    def clear(p, carry):
        outgoing[p] = unused
        return carry

    lax.fori_loop(0, boxes, clear, 0)

    def finish(b, carry):
        where = moved_from[b]
        box = where >> 8
        rank = where & 255
        recent = arrived[box, pl.ds(rank, 3, stride=cap), :]
        older = arrived[box, pl.ds(3 * cap + rank, 3, stride=cap), :]
        rows = pl.ds(b, 3, stride=blocks)
        now = speed[rows, :]
        stepped = positions[rows, :] + time_step * (23.0 * now - 16.0 * recent + 5.0 * older) / 12.0
        new_positions[rows, :] = stepped
        for axis in range(3):
            new_history[b, axis, 0:1, :] = now[axis : axis + 1]
            new_history[b, axis, 1:2, :] = recent[axis : axis + 1]
        out = age_place[b]
        outgoing[out >> 8, pl.ds(out & 255, 3, stride=cap), :] = stepped
        return carry

    lax.fori_loop(0, blocks, finish, 0, unroll=4)


def frame_kernel(blocks, cap, aged_from, arrived, tables, frame):
    def one(b, carry):
        where = aged_from[b]
        aged = arrived[where >> 8, pl.ds(where & 255, 3, stride=cap), :]
        cosine, sine, hub0, hub1, hub2 = [tables[n, pl.ds(b, 1), :] for n in range(5)]
        first = aged[0:1] - hub0
        second = aged[1:2] - hub1
        frame[pl.ds(b, 1), :] = cosine * first + sine * second
        frame[pl.ds(blocks + b, 1), :] = cosine * second - sine * first
        frame[pl.ds(2 * blocks + b, 1), :] = aged[2:3] - hub2
        return carry

    lax.fori_loop(0, blocks, one, 0, unroll=8)


def swap(values):
    return lax.all_to_all(values, "box", split_axis=0, concat_axis=0, tiled=True)


def call(kernel, name, in_specs, outs, scratch=(), limit=None):
    several = isinstance(outs, list)
    listed = outs if several else [outs]
    specs = [spec for spec, _, _ in listed]
    shapes = [jax.ShapeDtypeStruct(dims, dtype) for _, dims, dtype in listed]
    return pl.pallas_call(
        kernel,
        in_specs=in_specs,
        out_specs=specs if several else specs[0],
        out_shape=shapes if several else shapes[0],
        scratch_shapes=list(scratch),
        compiler_params=pltpu.CompilerParams(vmem_limit_bytes=limit),
        name=name,
    )


def body(
    positions,
    strengths,
    history,
    move_list,
    age_slot,
    fetch_list,
    tile_slot,
    tile_count,
    blade_id,
    hub_centre,
    azimuth,
):
    blocks = positions.shape[0]
    boxes = lax.axis_size("box")
    rcap = fetch_list.shape[2]
    kmax = tile_slot.shape[1]
    cap = 2 * blocks // boxes
    slots = boxes * rcap
    most = (blocks * kmax + slots) // 2 + UNROLL
    chunks, users, rows = plan_rows(slots, most)
    groups = slots // LANES

    places = jnp.transpose(positions, (1, 0, 2)).reshape(3 * blocks, LANES)
    gammas = jnp.transpose(strengths, (1, 0, 2)).reshape(3 * blocks, LANES)
    past = jnp.transpose(history, (0, 2, 1, 3))

    meta, move_place, age_place = call(
        functools.partial(meta_kernel, blocks, boxes, rcap, cap),
        "meta",
        [SMEM] * 3,
        [(SMEM, (boxes, LANES), I32), (SMEM, (blocks,), I32), (SMEM, (blocks,), I32)],
        [pltpu.SMEM((2 * boxes,), I32)],
    )(move_list, age_slot, fetch_list[0].T)
    labels = swap(meta)
    plan, ranked = call(
        functools.partial(plan_kernel, blocks, kmax, slots, most),
        "plan",
        [VMEM] * 2,
        [(VMEM, (rows, LANES), I32), (VMEM, (groups * (kmax + 8), LANES), I32)],
    )(tile_slot.T, tile_count.reshape(1, blocks))
    targets, centre, tables = call(
        functools.partial(target_kernel, blocks),
        "target_features",
        [VMEM, VMEM, SMEM, SMEM],
        [(VMEM, (blocks, LANES, LANES), BF), (VMEM, (8, LANES), F32), (VMEM, (5, blocks, LANES), F32)],
        [pltpu.VMEM((2 * 24 * 8, LANES), F32)],
    )(places, blade_id, hub_centre.T, azimuth)
    labels, plan, ranked, targets, centre, tables = lax.optimization_barrier(
        (labels, plan, ranked, targets, centre, tables)
    )
    answers = call(
        functools.partial(answer_kernel, blocks, boxes, rcap),
        "answer",
        [SMEM, VMEM, VMEM],
        (VMEM, (boxes, 6 * rcap, LANES), F32),
    )(labels, places, gammas)
    late_labels, late_past, answers = lax.optimization_barrier((labels, past, answers))
    fetched = swap(answers)
    packed_history, moved_from, aged_from = call(
        functools.partial(history_kernel, blocks, boxes, rcap, cap),
        "pack_history",
        [SMEM, SMEM, VMEM],
        [(VMEM, (boxes, 6 * cap, LANES), F32), (SMEM, (blocks,), I32), (SMEM, (blocks,), I32)],
    )(move_place, late_labels, late_past)
    fetched, packed_history = lax.optimization_barrier((fetched, packed_history))
    arrived = swap(packed_history)
    speed = call(
        functools.partial(velocity_kernel, blocks, boxes, rcap, slots, kmax, most),
        "velocity",
        [SMEM] * 2 + [VMEM] * 4,
        (VMEM, (3 * blocks, LANES), F32),
        [
            pltpu.VMEM((boxes, 24 * 8, LANES), F32),
            pltpu.VMEM((boxes, 64, LANES), F32),
            pltpu.VMEM((slots, LANES, LANES), BF),
            pltpu.VMEM((slots, 16, 2 * LANES), BF),
            pltpu.VMEM((blocks * 8, LANES), F32),
            pltpu.VMEM((blocks * 8, LANES), F32),
            pltpu.VMEM((UNROLL, 8, 2 * LANES), F32),
        ],
        48 << 20,
    )(plan, ranked, fetched, places, targets, centre)
    new_positions, new_history, outgoing = call(
        functools.partial(step_kernel, blocks, boxes, cap),
        "step",
        [SMEM] * 2 + [VMEM] * 3,
        [
            (VMEM, (3 * blocks, LANES), F32),
            (VMEM, (blocks, 3, 2, LANES), F32),
            (VMEM, (boxes, 3 * cap, LANES), F32),
        ],
    )(moved_from, age_place, arrived, places, speed)
    aged = swap(outgoing)
    frame = call(
        functools.partial(frame_kernel, blocks, cap),
        "frame",
        [SMEM, VMEM, VMEM],
        (VMEM, (3 * blocks, LANES), F32),
    )(aged_from, aged, tables)

    def back(rows):
        return jnp.transpose(rows.reshape(3, blocks, LANES), (1, 0, 2))

    return back(new_positions), jnp.transpose(new_history, (0, 2, 1, 3)), back(frame)


def solution(mesh):
    split = ("cases", "box")
    placed = (
        P(split, None, None),
        P(split, None, None),
        P(split, None, None, None),
        P(split),
        P(split),
        P(split, None, None),
        P(split, None),
        P(split),
        P(split, None),
        P("cases", None),
        P("cases"),
    )
    return jax.shard_map(
        body,
        mesh=mesh,
        in_specs=placed,
        out_specs=(P(split, None, None), P(split, None, None, None), P(split, None, None)),
        check_vma=False,
    )
```

time: 106 us -> 86.3 us (0.81); the launches traced: 104 us -> 85.5 us
  blocking collectives: 0 us -> 16.7 us
  Pallas kernels: 50.3 us -> 40 us
  local copies, waits for them, and re-layouts: 12 us -> 2.01 us
  waiting for transfers between devices: 18.7 us -> 10.1 us
  starting transfers between devices: 21.5 us -> 15.9 us
    all_to_all x0 -> x1, blocking collectives: none -> 16.7 us  [swap(): lax.all_to_all(values, 'box', split_axis=0, concat_axis=0, tiled=True)]
    pallas_call x8, Pallas kernels: 50.3 us -> 40 us  [the longest x1 22.3 us: body(): call(functools.partial(velocity_kernel, blocks, boxes, rcap, slots, kmax,...]
    unnamed x40 -> x16, local copies, waits for them, and re-layouts: 10.6 us -> 2.01 us
    all_to_all x4 -> x3, waiting for transfers between devices: 18.7 us -> 10.1 us  [swap(): lax.all_to_all(values, 'box', split_axis=0, concat_axis=0, tiled=True)]
    all_to_all x4 -> x3, starting transfers between devices: 21.5 us -> 15.9 us  [swap(): lax.all_to_all(values, 'box', split_axis=0, concat_axis=0, tiled=True)]
    squeeze x1 -> x0, local copies, waits for them, and re-layouts: 1.36 us -> none  [body(): fetch_list[0]]
  transfers between devices with their start and end apart: 4 -> 3, of which waited for: 3 -> 2; matrix products, arithmetic and copies ran while one was open for 6% -> 0% of each run, Pallas kernels for 18% -> 36%
where the time goes in v2:
time: 86.3 us; the launch traced here: 85.5 us
  Pallas kernels  40 us (46%)
  blocking collectives  16.7 us (19%)
  starting transfers between devices  15.9 us (18%)
  waiting for transfers between devices  10.1 us (12%)
  local copies, waits for them, and re-layouts  2.01 us (2%)
    pallas_call x1, Pallas kernels, body(): call(functools.partial(velocity_kernel, blocks, boxes, rcap, slots, kmax,...  22.3 us
    all_to_all x1, blocking collectives, swap(): lax.all_to_all(values, 'box', split_axis=0, concat_axis=0, tiled=True)  16.7 us
    all_to_all x3, starting transfers between devices, swap(): lax.all_to_all(values, 'box', split_axis=0, concat_axis=0, tiled=True)  15.9 us
    all_to_all x3, waiting for transfers between devices, swap(): lax.all_to_all(values, 'box', split_axis=0, concat_axis=0, tiled=True)  10.1 us
    pallas_call x1, Pallas kernels, body(): call(functools.partial(history_kernel, blocks, boxes, rcap, cap), 'pack_h...  3.11 us
    pallas_call x1, Pallas kernels, body(): call(functools.partial(target_kernel, blocks), 'target_features', [VMEM,...  2.8 us
    pallas_call x1, Pallas kernels, body(): call(functools.partial(meta_kernel, blocks, boxes, rcap, cap), 'meta', [S...  2.78 us
    pallas_call x1, Pallas kernels, body(): call(functools.partial(plan_kernel, blocks, kmax, slots, most), 'plan', [...  2.46 us
  transfers between devices with their start and end apart: 3, of which 2 were waited for; matrix products, arithmetic and copies ran while one was open for 0% of the time, Pallas kernels for 36%

profile of v2, /device:TPU:0, one launch (start us, length us, event | category | flops | bytes accessed | tf_op | source)
XLA Modules:
  0.0 85.5 jit_solution(18354942686700503948)
XLA Ops:
  0.6 0.0 copy-start.1
  0.6 2.8 %meta.1 = (s32[16,128]{1,0:T(8,128)}, s32[64]{0:T(128)}, s32[64]{0:T(128)}) custom-call(s32[64]{0:T(128)} %move.1, s32[64]{0:T(128)} %age.1, s32[8,16]{1,0:T(8,128)} %bitcast.35), custom_call_target="tpu_custom_call" | custom-call | tf_op jit(solution)/shard_map/meta/pallas_call | solution.py:426
  3.4 7.4 %all-to-all-start = ((s32[16,1,128]{2,1,0:T(1,128)}), s32[16,1,128]{2,1,0:T(1,128)S(1)}, u32[]{:S(2)}, u32[]{:S(2)}) async-start(s32[16,1,128]{2,1,0:T(1,128)} %bitcast.34), calls=%async_computation | async-start | bytes 16384 | tf_op jit(solution)/shard_map/all_to_all | solution.py:380
  10.8 2.5 %plan.1 = (s32[16,128]{1,0:T(8,128)}, s32[40,128]{1,0:T(8,128)}) custom-call(s32[32,64]{1,0:T(8,128)} %bitcast.33, s32[1,64]{1,0:T(1,128)} %bitcast.37), custom_call_target="tpu_custom_call" | custom-call | tf_op jit(solution)/shard_map/plan/pallas_call | solution.py:434
  13.3 0.0 copy-start.3
  13.3 0.0 copy-start.4
  13.3 2.8 %target_features.1 = (bf16[64,128,128]{2,1,0:T(8,128)(2,1)}, f32[8,128]{1,0:T(8,128)}, f32[5,64,128]{2,1,0:T(8,128)}) custom-call(f32[192,128]{1,0:T(8,128)} %bitcast.24, s32[64,128]{1,0:T(8,128)} %blade.1, f32[3,6]{1,0:T(4,128)} %bitcast.36, f32[6]{0:T(128)} %azimuth.1), custom_call_target="tpu_custom_call" | custom-call | tf_op jit(solution)/shard_map/target_features/pallas_call | solution.py:440
  16.1 0.0 copy-start
  16.1 0.0 copy-start.5
  16.1 1.1 %all-to-all-done = s32[16,1,128]{2,1,0:T(1,128)S(1)} async-done(((s32[16,1,128]{2,1,0:T(1,128)}), s32[16,1,128]{2,1,0:T(1,128)S(1)}, u32[]{:S(2)}, u32[]{:S(2)}) %all-to-all-start) | async-done | bytes 8224 | tf_op jit(solution)/shard_map/all_to_all | solution.py:380
  17.2 0.0 copy-start.7
  17.2 0.6 copy-done.7
  17.8 2.3 %answer.1 = f32[16,48,128]{2,1,0:T(8,128)} custom-call(s32[16,128]{1,0:T(8,128)} %bitcast.31, f32[192,128]{1,0:T(8,128)} %bitcast.25, f32[192,128]{1,0:T(8,128)} %bitcast.29), custom_call_target="tpu_custom_call" | custom-call | tf_op jit(solution)/shard_map/answer/pallas_call | solution.py:450
  20.0 5.0 %all-to-all-start.1 = ((f32[16,48,128]{2,1,0:T(8,128)}), f32[16,48,128]{2,1,0:T(8,128)S(1)}, u32[]{:S(2)}, u32[]{:S(2)}) async-start(f32[16,48,128]{2,1,0:T(8,128)} %answer.1), calls=%async_computation.1 | async-start | bytes 786432 | tf_op jit(solution)/shard_map/all_to_all | solution.py:380
  25.0 3.1 %pack_history.1 = (f32[16,48,128]{2,1,0:T(8,128)}, s32[64]{0:T(128)}, s32[64]{0:T(128)}) custom-call(s32[64]{0:T(128)} %get-tuple-element.28.place, s32[16,128]{1,0:T(8,128)} %bitcast.32, f32[64,3,2,128]{3,2,1,0:T(2,128)} %bitcast.28), custom_call_target="tpu_custom_call" | custom-call | tf_op jit(solution)/shard_map/pack_history/pallas_call | solution.py:458
  28.1 9.1 %all-to-all-done.1.fetched = f32[16,48,128]{2,1,0:T(8,128)S(1)} async-done(((f32[16,48,128]{2,1,0:T(8,128)}), f32[16,48,128]{2,1,0:T(8,128)S(1)}, u32[]{:S(2)}, u32[]{:S(2)}) %all-to-all-start.1) | async-done | bytes 393248 | tf_op jit(solution)/shard_map/all_to_all | solution.py:380
  37.2 3.6 %all-to-all-start.2 = ((f32[16,48,128]{2,1,0:T(8,128)}), f32[16,48,128]{2,1,0:T(8,128)S(1)}, u32[]{:S(2)}, u32[]{:S(2)}) async-start(f32[16,48,128]{2,1,0:T(8,128)} %get-tuple-element.42), calls=%async_computation.2 | async-start | bytes 786432 | tf_op jit(solution)/shard_map/all_to_all | solution.py:380
  40.8 0.0 copy-done.1
  40.8 0.0 copy-done.3
  40.8 0.0 copy-done.4
  40.8 0.0 copy-done
  40.8 0.0 copy-done.5
  40.8 22.3 %velocity.1.speed = f32[192,128]{1,0:T(8,128)S(1)} custom-call(s32[16,128]{1,0:T(8,128)S(1)} %copy-done.4, s32[40,128]{1,0:T(8,128)S(1)} %copy-done.3, f32[16,48,128]{2,1,0:T(8,128)S(1)} %all-to-all-done.1.fetched, f32[192,128]{1,0:T(8,128)S(1)} %bitcast.27, bf16[64,128,128]{2,1,0:T(8,128)(2,1)S(1)} %copy-done, f32[8,128]{1,0:T(8,128)S(1)} %copy-done.5), custom_call_target="tpu_custom_call" | custom-call | tf_op jit(solution)/shard_map/velocity/pallas_call | solution.py:466
  63.1 0.0 copy-start.2
  63.1 0.6 copy-done.2
  63.8 0.0 all-to-all-done.2.arrived
  63.8 0.0 copy-start.6
  63.8 0.8 copy-done.6
  64.5 2.4 %step.1 = (f32[192,128]{1,0:T(8,128)}, f32[64,3,2,128]{3,2,1,0:T(2,128)}, f32[16,24,128]{2,1,0:T(8,128)}) custom-call(s32[64]{0:T(128)} %get-tuple-element.38.moved_from, s32[64]{0:T(128)} %get-tuple-element.39.age_place, f32[16,48,128]{2,1,0:T(8,128)} %copy-done.6, f32[192,128]{1,0:T(8,128)} %bitcast.26, f32[192,128]{1,0:T(8,128)} %copy-done.2), custom_call_target="tpu_custom_call" | custom-call | tf_op jit(solution)/shard_map/step/pallas_call | solution.py:482
  66.9 16.7 %all_to_all.27.arrived = f32[16,24,128]{2,1,0:T(8,128)} all-to-all(f32[16,24,128]{2,1,0:T(8,128)} %get-tuple-element.51), channel_id=1, replica_groups=mesh['cases'=2,'box'=16] {'box'}, dimensions={0} | all-to-all | bytes 393216 | tf_op jit(solution)/shard_map/all_to_all | solution.py:380
  83.7 1.9 %frame.1 = f32[192,128]{1,0:T(8,128)} custom-call(s32[64]{0:T(128)} %get-tuple-element.50.aged_from, f32[16,24,128]{2,1,0:T(8,128)} %all_to_all.27.arrived, f32[5,64,128]{2,1,0:T(8,128)} %get-tuple-element.52.tables), custom_call_target="tpu_custom_call" | custom-call | tf_op jit(solution)/shard_map/frame/pallas_call | solution.py:493
Async XLA Ops:
  0.6 40.1 %copy-start.1 = (f32[64,3,128]{2,0,1:T(8,128)S(1)}, f32[64,3,128]{2,0,1:T(8,128)}, u32[]{:S(2)}) copy-start(f32[64,3,128]{2,0,1:T(8,128)} %param.11) | copy-start | bytes 294916
  3.4 13.7 %all-to-all-start = ((s32[16,1,128]{2,1,0:T(1,128)}), s32[16,1,128]{2,1,0:T(1,128)S(1)}, u32[]{:S(2)}, u32[]{:S(2)}) async-start(s32[16,1,128]{2,1,0:T(1,128)} %bitcast.34), calls=%async_computation | async-start | bytes 16384 | tf_op jit(solution)/shard_map/all_to_all | solution.py:380
  13.3 27.5 %copy-start.3 = (s32[40,128]{1,0:T(8,128)S(1)}, s32[40,128]{1,0:T(8,128)}, u32[]{:S(2)}) copy-start(s32[40,128]{1,0:T(8,128)} %get-tuple-element.44.ranked) | copy-start | bytes 61444
  13.3 27.5 %copy-start.4 = (s32[16,128]{1,0:T(8,128)S(1)}, s32[16,128]{1,0:T(8,128)}, u32[]{:S(2)}) copy-start(s32[16,128]{1,0:T(8,128)} %get-tuple-element.43.plan) | copy-start | bytes 24580
  16.1 24.7 %copy-start = (bf16[64,128,128]{2,1,0:T(8,128)(2,1)S(1)}, bf16[64,128,128]{2,1,0:T(8,128)(2,1)}, u32[]{:S(2)}) copy-start(bf16[64,128,128]{2,1,0:T(8,128)(2,1)} %get-tuple-element.46.targets) | copy-start | bytes 6291460
  16.1 24.7 %copy-start.5 = (f32[8,128]{1,0:T(8,128)S(1)}, f32[8,128]{1,0:T(8,128)}, u32[]{:S(2)}) copy-start(f32[8,128]{1,0:T(8,128)} %get-tuple-element.47.centre) | copy-start | bytes 12292
  17.2 0.6 copy-start.7
  20.0 17.2 %all-to-all-start.1 = ((f32[16,48,128]{2,1,0:T(8,128)}), f32[16,48,128]{2,1,0:T(8,128)S(1)}, u32[]{:S(2)}, u32[]{:S(2)}) async-start(f32[16,48,128]{2,1,0:T(8,128)} %answer.1), calls=%async_computation.1 | async-start | bytes 786432 | tf_op jit(solution)/shard_map/all_to_all | solution.py:380
  37.2 26.6 %all-to-all-start.2 = ((f32[16,48,128]{2,1,0:T(8,128)}), f32[16,48,128]{2,1,0:T(8,128)S(1)}, u32[]{:S(2)}, u32[]{:S(2)}) async-start(f32[16,48,128]{2,1,0:T(8,128)} %get-tuple-element.42), calls=%async_computation.2 | async-start | bytes 786432 | tf_op jit(solution)/shard_map/all_to_all | solution.py:380
  63.1 0.6 copy-start.2
  63.8 0.8 copy-start.6

commit v3 on v2

v3 whole, which is shorter than its diff:
```python
import functools
import math

import jax
import jax.numpy as jnp
from jax import lax
from jax.experimental import pallas as pl
from jax.experimental.pallas import tpu as pltpu
from jax.sharding import PartitionSpec as P

ROTORS = 6
BLADES = 3

core_square = 0.05
time_step = 0.05

LANES = 128
FEATURES = 32
UNROLL = 32
BUILD = 8
BF = jnp.bfloat16
F32 = jnp.float32
I32 = jnp.int32

SMEM = pl.BlockSpec(memory_space=pltpu.SMEM)
VMEM = pl.BlockSpec(memory_space=pltpu.VMEM)
ANY = pl.BlockSpec(memory_space=pl.ANY)


def split3(value):
    high = value.astype(BF).astype(F32)
    rest = value - high
    middle = rest.astype(BF).astype(F32)
    return high, middle, rest - middle


def iota(dims, axis):
    return lax.broadcasted_iota(I32, dims, axis)


def meta_kernel(blocks, boxes, rcap, cap, move, age, fetch, meta, move_place, age_place, fill):
    def ask(p, carry):
        for lane in range(rcap):
            meta[p, lane] = fetch[lane, p]
        fill[p] = 0
        fill[boxes + p] = 0
        return carry

    lax.fori_loop(0, boxes, ask, 0, unroll=4)

    def place(g, carry):
        for source, first, target, lane in (
            (move, 0, move_place, rcap),
            (age, boxes, age_place, rcap + cap),
        ):
            block = source[g]
            box = lax.div(block, blocks)
            rank = fill[first + box]
            fill[first + box] = rank + 1
            meta[box, lane + rank] = block - box * blocks
            target[g] = box * 256 + rank
        return carry

    lax.fori_loop(0, blocks, place, 0, unroll=4)

    def number(p, carry):
        meta[p, rcap + 2 * cap] = fill[p]
        meta[p, rcap + 2 * cap + 1] = fill[boxes + p]
        return carry

    lax.fori_loop(0, boxes, number, 0, unroll=4)


def plan_rows(slots, most):
    chunks = (most + LANES - 1) // LANES
    users = (slots + BUILD + LANES - 1) // LANES
    return chunks, users, (2 * chunks + users + 3 + 7) // 8 * 8


def plan_kernel(blocks, kmax, rcap, cap, slots, most, place, history, tiles, count,
                message, plan, ranked, packed, sem):
    def one(g, carry):
        where = place[g]
        box = where >> 8
        rank = where & 255
        for axis in range(3):
            packed[box, pl.ds(axis * cap + rank, 2, stride=3 * cap), :] = history[g, axis]
        return carry

    lax.fori_loop(0, blocks, one, 0, unroll=8)
    sent = pltpu.make_async_copy(packed, message.at[:, pl.ds(6 * rcap, packed.shape[1]), :], sem)
    sent.start()
    half = kmax
    near = 2 * rcap
    chunks, users, rows = plan_rows(slots, most)
    turn = lax.axis_index("box") * rcap
    slot = iota((slots, blocks), 0) ^ turn
    times = jnp.zeros((slots, blocks), I32)
    for k in range(kmax):
        named = jnp.where(count[...] > k, tiles[k : k + 1, :], -1)
        times = times + jnp.where(slot == named, 1, 0)
    present = jnp.where(times > 0, 1.0, 0.0)
    inner = jnp.where(iota((blocks, blocks), 0) < iota((blocks, blocks), 1), 1.0, 0.0)
    rank = jnp.dot(present.astype(BF), inner.astype(BF), preferred_element_type=F32)
    rank = jnp.where(times > 0, rank, -2.0)
    number = jnp.dot(
        present.astype(BF), jnp.ones((blocks, LANES), BF), preferred_element_type=F32
    ).astype(I32)
    pairs = (number + 1) >> 1
    outer = jnp.where(iota((slots, slots), 1) <= iota((slots, slots), 0), 1.0, 0.0).astype(BF)
    ends = jnp.dot(outer, pairs.astype(F32).astype(BF), preferred_element_type=F32).astype(I32)
    used = jnp.where(number > 0, 1.0, 0.0).astype(BF)
    tally = jnp.dot(outer, used, preferred_element_type=F32).astype(I32)
    lane = iota((1, LANES), 1)

    def first_after(done):
        return jnp.sum(jnp.where(tally <= done, 1, 0), axis=0, keepdims=True)

    begin = jnp.zeros((1, LANES), I32)
    behind = jnp.zeros((1, LANES), I32)
    for part, last in ((0, near), (1, slots)):
        stop = ends[last - 1 : last, :]
        opening = first_after(behind)
        for chunk in range(chunks):
            spot = begin + lane + chunk * LANES
            past = ends <= spot
            source = jnp.sum(jnp.where(past, 1, 0), axis=0, keepdims=True)
            start = jnp.max(jnp.where(past, ends, 0), axis=0, keepdims=True)
            word = jnp.where(spot < stop, source + (spot - start) * 65536, opening + half * 65536)
            row = part * chunks + chunk
            plan[row : row + 1, :] = word
        row = rows - 3 + part
        plan[row : row + 1, :] = (stop - begin + (UNROLL - 1)) >> (UNROLL.bit_length() - 1)
        if part == 0:
            begin = stop
            behind = tally[last - 1 : last, :]
    live = tally[slots - 1 : slots, :]
    for chunk in range(users):
        spot = behind + lane + chunk * LANES
        row = 2 * chunks + chunk
        plan[row : row + 1, :] = jnp.where(spot < live, first_after(spot), first_after(behind))
    plan[rows - 1 : rows, :] = (live - behind + (BUILD - 1)) >> (BUILD.bit_length() - 1)
    limit = jnp.max(pairs)
    for group in range(slots // LANES):
        at = slice(group * LANES, (group + 1) * LANES)
        wide = [
            jnp.concatenate([value, jnp.zeros((LANES, LANES - blocks), F32)], axis=1).T[:blocks]
            for value in (rank[at], times[at].astype(F32))
        ]
        position = wide[0].astype(I32)
        entry = iota((blocks, LANES), 0) + wide[1].astype(I32) * 256
        entry = jnp.where((position & 1) == 1, entry * 65536, entry)
        position = position >> 1
        first = group * (half + 8)
        ranked[first + half : first + half + 8, :] = jnp.zeros((8, LANES), I32)

        def fill(t, carry):
            found = jnp.sum(jnp.where(position == t, entry, 0), axis=0, keepdims=True)
            ranked[pl.ds(first + t, 1), :] = found
            return carry

        lax.fori_loop(0, limit, fill, 0)
    sent.wait()


def target_features(blocks, positions, blade, hub, azimuth, feats, centre, tables, stage):
    middle = [
        jnp.sum(positions[axis * blocks : (axis + 1) * blocks, :], axis=(0, 1), keepdims=True)
        / (blocks * LANES)
        for axis in range(3)
    ]
    for axis in range(3):
        centre[axis : axis + 1, :] = jnp.broadcast_to(middle[axis], (1, LANES))
    ones = jnp.ones((8, LANES), F32)
    pad = jnp.zeros((FEATURES - 24, LANES), F32)
    for group in range(blocks // 8):
        first = group * 8
        at = [
            positions[axis * blocks + first : axis * blocks + first + 8, :] - middle[axis]
            for axis in range(3)
        ]
        norm = split3(at[0] * at[0] + at[1] * at[1] + at[2] * at[2] + core_square)
        parts = [split3(-2.0 * value) for value in at]
        rows = []
        for piece in (0, 1, 2, 0, 1, 0):
            rows += [parts[axis][piece] for axis in range(3)]
        rows += [ones, ones, ones, norm[0], norm[1], norm[2]]
        base = (group % 2) * 24 * 8
        for f, value in enumerate(rows):
            stage[base + f * 8 : base + f * 8 + 8, :] = value
        for t in range(8):
            picked = stage[pl.ds(base + t, 24, stride=8), :]
            feats[first + t] = jnp.concatenate([picked, pad], axis=0).astype(BF)
    lane = iota((8, LANES), 1)
    angle = jnp.zeros((8, LANES), F32)
    hubs = [jnp.zeros((8, LANES), F32) for _ in range(3)]
    for q in range(ROTORS * BLADES):
        turn = F32(2.0 * math.pi) * F32(q % BLADES) / F32(BLADES)
        angle = jnp.where(lane == q, azimuth[q // BLADES] + turn, angle)
        for axis in range(3):
            hubs[axis] = jnp.where(lane == q, hub[axis, q // BLADES], hubs[axis])
    sources = [jnp.cos(angle), jnp.sin(angle)] + hubs
    for group in range(blocks // 8):
        index = blade[group * 8 : group * 8 + 8, :]
        for n, source in enumerate(sources):
            tables[n, group * 8 : group * 8 + 8, :] = jnp.take_along_axis(source, index, axis=1)


def answer_kernel(blocks, boxes, rcap, asked, positions, strengths, _, message, packed, sems):
    quarter = boxes // 4
    sent = []
    for part in range(4):
        first = part * quarter

        def one(p, carry):
            for i in range(rcap):
                block = jnp.maximum(asked[p, i], 0)
                packed[p, pl.ds(i, 3, stride=rcap), :] = positions[pl.ds(block, 3, stride=blocks), :]
                packed[p, pl.ds(3 * rcap + i, 3, stride=rcap), :] = strengths[
                    pl.ds(block, 3, stride=blocks), :
                ]
            return carry

        lax.fori_loop(first, first + quarter, one, 0)
        peers = pl.ds(first, quarter)
        copy = pltpu.make_async_copy(
            packed.at[peers], message.at[peers, pl.ds(0, 6 * rcap), :], sems.at[part]
        )
        copy.start()
        sent.append(copy)
    for copy in sent:
        copy.wait()


def prepare(source, centre, rcap, stage, table_stage, o):
    ones = jnp.ones((8, LANES), F32)
    zeros = jnp.zeros((8, LANES), F32)
    at = [source(axis) - centre[axis : axis + 1, :] for axis in range(3)]
    gamma = [source(3 + axis) for axis in range(3)]
    parts = [split3(value) for value in at]
    norm = split3(at[0] * at[0] + at[1] * at[1] + at[2] * at[2])
    values = []
    for piece in (0, 0, 0, 1, 1, 2):
        values += [parts[axis][piece] for axis in range(3)]
    values += [norm[0], norm[1], norm[2], ones, ones, ones]
    for f, value in enumerate(values):
        stage[o, f * 8 : f * 8 + 8, :] = value
    for axis in range(3):
        left, right = (axis + 1) % 3, (axis + 2) % 3
        table_stage[o, axis * 8 : axis * 8 + 8, :] = gamma[axis]
        table_stage[o, (3 + axis) * 8 : (4 + axis) * 8, :] = (
            at[left] * gamma[right] - at[right] * gamma[left]
        )
    table_stage[o, 48:56, :] = zeros
    table_stage[o, 56:64, :] = zeros


def build(slot, identity, stage, table_stage, feats, tables):
    zeros = jnp.zeros((8, LANES), F32)
    pad = jnp.zeros((LANES - 24, LANES), F32)
    o = slot >> 3
    i = slot & 7
    picked = jnp.concatenate([stage[o, pl.ds(i, 24, stride=8), :], pad], axis=0)
    turned = lax.dot_general(
        identity, picked.astype(BF), (((1,), (1,)), ((), ())), preferred_element_type=F32
    )
    feats[slot] = turned.astype(BF)
    table = table_stage[o, pl.ds(i, 8, stride=8), :]
    high = table.astype(BF).astype(F32)
    left = jnp.concatenate([high, table - high], axis=0)
    right = jnp.concatenate([high, zeros], axis=0)
    tables[slot] = jnp.concatenate([left, right], axis=1).astype(BF)


def unit():
    return jnp.where(iota((LANES, LANES), 0) == iota((LANES, LANES), 1), 1.0, 0.0).astype(BF)


def gather_pairs(first, number, slots, half, plan, ranked, targets, feats, tables, sums0, sums1, held):
    held[...] = jnp.zeros_like(held)
    empty = jnp.zeros((LANES - FEATURES, 2 * LANES), BF)

    def named(it):
        found = []
        for u in range(UNROLL):
            at = it * UNROLL + u
            word = plan[first + (at >> 7), at & 127]
            slot = word & 65535
            row = word >> 16
            if slots > LANES:
                row = row + (slot >> 7) * (half + 8)
            found.append((slot, ranked[row, slot & 127]))
        return found

    def flush(it):
        for u, (_, pair) in enumerate(named(it)):
            for sums, word, part in (
                (sums0, pair & 65535, held[u, :, :LANES]),
                (sums1, pair >> 16, held[u, :, LANES:]),
            ):
                at = pl.ds(pl.multiple_of((word & 255) * 8, 8), 8)
                sums[at, :] = sums[at, :] + (word >> 8).astype(F32) * part

    def accumulate(it, carry):
        flush(jnp.maximum(it - 1, 0))
        for u, (slot, pair) in enumerate(named(it)):
            both = jnp.concatenate([targets[pair & 255], targets[(pair >> 16) & 255]], axis=1)
            both = jnp.concatenate([both, empty], axis=0)
            inverse = lax.rsqrt(jnp.dot(feats[slot], both, preferred_element_type=F32))
            weight = inverse * inverse * inverse
            high = weight.astype(BF)
            low = (weight - high.astype(F32)).astype(BF)
            summed = jnp.dot(
                tables[slot], jnp.concatenate([high, low], axis=0), preferred_element_type=F32
            )
            held[u] = summed[:8] + summed[8:]
        return carry

    lax.fori_loop(0, number, accumulate, 0)

    @pl.when(number > 0)
    def _():
        flush(number - 1)


def near_kernel(blocks, boxes, rcap, cap, slots, half, most, plan, ranked, asked, labels, hub,
                azimuth, places, gammas, mate_places, mate_gammas, blade,
                partial, targets, centre, turns, moved_from, aged_from,
                target_stage, local, stage, table_stage, feats, tables, sums0, sums1, held):
    target_features(blocks, places, blade, hub, azimuth, targets, centre, turns, target_stage)

    def peer(p, carry):
        for target, lane, number in ((moved_from, rcap, 0), (aged_from, rcap + cap, 1)):

            def label(rank, carry):
                target[labels[p, lane + rank]] = p * 256 + rank
                return carry

            lax.fori_loop(0, labels[p, rcap + 2 * cap + number], label, 0)
        return carry

    lax.fori_loop(0, boxes, peer, 0)
    _, _, rows = plan_rows(slots, most)
    me = lax.axis_index("box")
    for o, (from_places, from_gammas) in enumerate(((places, gammas), (mate_places, mate_gammas))):
        for i in range(rcap):
            block = jnp.maximum(asked[i, me ^ o], 0)
            local[o, pl.ds(i, 3, stride=rcap), :] = from_places[pl.ds(block, 3, stride=blocks), :]
            local[o, pl.ds(3 * rcap + i, 3, stride=rcap), :] = from_gammas[
                pl.ds(block, 3, stride=blocks), :
            ]
    for o in range(2):
        prepare(
            lambda c: local[o, c * rcap : (c + 1) * rcap, :], centre, rcap, stage, table_stage, o
        )
    identity = unit()
    for slot in range(2 * rcap):
        build(slot, identity, stage, table_stage, feats, tables)
    sums0[...] = jnp.zeros_like(sums0)
    sums1[...] = jnp.zeros_like(sums1)
    gather_pairs(
        0, plan[rows - 3, 0], slots, half, plan, ranked, targets, feats, tables, sums0, sums1, held
    )
    partial[...] = sums0[...] + sums1[...]


def far_kernel(blocks, boxes, rcap, cap, slots, half, most, plan, ranked, moved_from, age_place,
               fetched, positions, targets, centre, partial,
               new_positions, new_history, outgoing,
               speed, stage, table_stage, feats, tables, sums0, sums1, held):
    chunks, _, rows = plan_rows(slots, most)
    me = lax.axis_index("box")

    def owner(o, carry):
        at = o ^ me
        prepare(
            lambda c: fetched[at, c * rcap : (c + 1) * rcap, :], centre, rcap, stage, table_stage, o
        )
        return carry

    lax.fori_loop(2, boxes, owner, 0, unroll=2)
    identity = unit()

    def several(it, carry):
        for u in range(BUILD):
            at = it * BUILD + u
            slot = plan[2 * chunks + (at >> 7), at & 127]
            build(slot, identity, stage, table_stage, feats, tables)
        return carry

    lax.fori_loop(0, plan[rows - 1, 0], several, 0)
    sums0[...] = partial[...]
    sums1[...] = jnp.zeros_like(sums1)
    gather_pairs(
        chunks, plan[rows - 2, 0], slots, half, plan, ranked, targets, feats, tables,
        sums0, sums1, held,
    )
    scale = 1.0 / (4.0 * math.pi)
    for group in range(blocks // 8):
        first = group * 8
        total = [
            sums0[pl.ds(first * 8 + f, 8, stride=8), :] + sums1[pl.ds(first * 8 + f, 8, stride=8), :]
            for f in range(6)
        ]
        at = [
            positions[axis * blocks + first : axis * blocks + first + 8, :]
            - centre[axis : axis + 1, :]
            for axis in range(3)
        ]
        for axis in range(3):
            left, right = (axis + 1) % 3, (axis + 2) % 3
            speed[axis * blocks + first : axis * blocks + first + 8, :] = scale * (
                at[left] * total[right] - at[right] * total[left] - total[3 + axis]
            )
    unused = jnp.zeros((3 * cap, LANES), F32)

    def clear(p, carry):
        outgoing[p] = unused
        return carry

    lax.fori_loop(0, boxes, clear, 0)

    def finish(b, carry):
        where = moved_from[b]
        box = where >> 8
        rank = where & 255
        recent = fetched[box, pl.ds(6 * rcap + rank, 3, stride=cap), :]
        older = fetched[box, pl.ds(6 * rcap + 3 * cap + rank, 3, stride=cap), :]
        rows = pl.ds(b, 3, stride=blocks)
        now = speed[rows, :]
        stepped = positions[rows, :] + time_step * (23.0 * now - 16.0 * recent + 5.0 * older) / 12.0
        new_positions[rows, :] = stepped
        for axis in range(3):
            new_history[b, axis, 0:1, :] = now[axis : axis + 1]
            new_history[b, axis, 1:2, :] = recent[axis : axis + 1]
        out = age_place[b]
        outgoing[out >> 8, pl.ds(out & 255, 3, stride=cap), :] = stepped
        return carry

    lax.fori_loop(0, blocks, finish, 0, unroll=4)


def frame_kernel(blocks, cap, aged_from, arrived, tables, frame):
    def one(b, carry):
        where = aged_from[b]
        aged = arrived[where >> 8, pl.ds(where & 255, 3, stride=cap), :]
        cosine, sine, hub0, hub1, hub2 = [tables[n, pl.ds(b, 1), :] for n in range(5)]
        first = aged[0:1] - hub0
        second = aged[1:2] - hub1
        frame[pl.ds(b, 1), :] = cosine * first + sine * second
        frame[pl.ds(blocks + b, 1), :] = cosine * second - sine * first
        frame[pl.ds(2 * blocks + b, 1), :] = aged[2:3] - hub2
        return carry

    lax.fori_loop(0, blocks, one, 0, unroll=8)


def swap(values):
    return lax.all_to_all(values, "box", split_axis=0, concat_axis=0, tiled=True)


def call(kernel, name, in_specs, outs, scratch=(), aliases={}):
    several = isinstance(outs, list)
    listed = outs if several else [outs]
    specs = [spec for spec, _, _ in listed]
    shapes = [jax.ShapeDtypeStruct(dims, dtype) for _, dims, dtype in listed]
    return pl.pallas_call(
        kernel,
        in_specs=in_specs,
        out_specs=specs if several else specs[0],
        out_shape=shapes if several else shapes[0],
        scratch_shapes=list(scratch),
        input_output_aliases=aliases,
        compiler_params=pltpu.CompilerParams(vmem_limit_bytes=60 << 20),
        name=name,
    )


def body(
    positions,
    strengths,
    history,
    move_list,
    age_slot,
    fetch_list,
    tile_slot,
    tile_count,
    blade_id,
    hub_centre,
    azimuth,
):
    blocks = positions.shape[0]
    boxes = lax.axis_size("box")
    rcap = fetch_list.shape[2]
    kmax = tile_slot.shape[1]
    cap = 2 * blocks // boxes
    slots = boxes * rcap
    most = (blocks * kmax + slots) // 2 + UNROLL
    chunks, users, rows = plan_rows(slots, most)
    groups = slots // LANES

    places = jnp.transpose(positions, (1, 0, 2)).reshape(3 * blocks, LANES)
    gammas = jnp.transpose(strengths, (1, 0, 2)).reshape(3 * blocks, LANES)
    past = jnp.transpose(history, (0, 2, 1, 3))

    asked = fetch_list[0].T
    meta, move_place, age_place = call(
        functools.partial(meta_kernel, blocks, boxes, rcap, cap),
        "meta",
        [SMEM] * 3,
        [(SMEM, (boxes, LANES), I32), (SMEM, (blocks,), I32), (SMEM, (blocks,), I32)],
        [pltpu.SMEM((2 * boxes,), I32)],
    )(move_list, age_slot, asked)
    labels = swap(meta)
    past_rows = (6 * cap + 7) // 8 * 8
    message_shape = (boxes, 6 * rcap + past_rows, LANES)
    message, plan, ranked = call(
        functools.partial(plan_kernel, blocks, kmax, rcap, cap, slots, most),
        "plan",
        [SMEM] + [VMEM] * 3,
        [
            (ANY, message_shape, F32),
            (VMEM, (rows, LANES), I32),
            (VMEM, (groups * (kmax + 8), LANES), I32),
        ],
        [pltpu.VMEM((boxes, past_rows, LANES), F32), pltpu.SemaphoreType.DMA],
    )(move_place, past, tile_slot.T, tile_count.reshape(1, blocks))
    mates = [(box, box ^ 1) for box in range(boxes)]
    mate_places = lax.ppermute(places, "box", mates)
    mate_gammas = lax.ppermute(gammas, "box", mates)
    labels, message, plan, ranked, mate_places, mate_gammas = lax.optimization_barrier(
        (labels, message, plan, ranked, mate_places, mate_gammas)
    )
    message = call(
        functools.partial(answer_kernel, blocks, boxes, rcap),
        "answer",
        [SMEM, VMEM, VMEM, ANY],
        (ANY, message_shape, F32),
        [pltpu.VMEM((boxes, 6 * rcap, LANES), F32), pltpu.SemaphoreType.DMA((4,))],
        {3: 0},
    )(labels, places, gammas, message)
    plan, ranked, mate_places, message = lax.optimization_barrier(
        (plan, ranked, mate_places, message)
    )
    fetched = swap(message)

    def scratch(owners):
        return [
            pltpu.VMEM((owners, 24 * 8, LANES), F32),
            pltpu.VMEM((owners, 64, LANES), F32),
            pltpu.VMEM((owners * rcap, LANES, LANES), BF),
            pltpu.VMEM((owners * rcap, 16, 2 * LANES), BF),
            pltpu.VMEM((blocks * 8, LANES), F32),
            pltpu.VMEM((blocks * 8, LANES), F32),
            pltpu.VMEM((UNROLL, 8, 2 * LANES), F32),
        ]

    partial, targets, centre, turns, moved_from, aged_from = call(
        functools.partial(near_kernel, blocks, boxes, rcap, cap, slots, kmax, most),
        "near",
        [SMEM] * 6 + [VMEM] * 5,
        [
            (VMEM, (blocks * 8, LANES), F32),
            (VMEM, (blocks, FEATURES, LANES), BF),
            (VMEM, (8, LANES), F32),
            (VMEM, (5, blocks, LANES), F32),
            (SMEM, (blocks,), I32),
            (SMEM, (blocks,), I32),
        ],
        [pltpu.VMEM((2 * 24 * 8, LANES), F32), pltpu.VMEM((2, 6 * rcap, LANES), F32)] + scratch(2),
    )(
        plan, ranked, asked, labels, hub_centre.T, azimuth,
        places, gammas, mate_places, mate_gammas, blade_id,
    )
    fetched, partial = lax.optimization_barrier((fetched, partial))
    new_positions, new_history, outgoing = call(
        functools.partial(far_kernel, blocks, boxes, rcap, cap, slots, kmax, most),
        "far",
        [SMEM] * 4 + [VMEM] * 5,
        [
            (VMEM, (3 * blocks, LANES), F32),
            (VMEM, (blocks, 3, 2, LANES), F32),
            (VMEM, (boxes, 3 * cap, LANES), F32),
        ],
        [pltpu.VMEM((3 * blocks, LANES), F32)] + scratch(boxes),
    )(plan, ranked, moved_from, age_place, fetched, places, targets, centre, partial)
    aged = swap(outgoing)
    frame = call(
        functools.partial(frame_kernel, blocks, cap),
        "frame",
        [SMEM, VMEM, VMEM],
        (VMEM, (3 * blocks, LANES), F32),
    )(aged_from, aged, turns)

    def back(rows):
        return jnp.transpose(rows.reshape(3, blocks, LANES), (1, 0, 2))

    return back(new_positions), jnp.transpose(new_history, (0, 2, 1, 3)), back(frame)


def solution(mesh):
    split = ("cases", "box")
    placed = (
        P(split, None, None),
        P(split, None, None),
        P(split, None, None, None),
        P(split),
        P(split),
        P(split, None, None),
        P(split, None),
        P(split),
        P(split, None),
        P("cases", None),
        P("cases"),
    )
    return jax.shard_map(
        body,
        mesh=mesh,
        in_specs=placed,
        out_specs=(P(split, None, None), P(split, None, None, None), P(split, None, None)),
        check_vma=False,
    )
```

time: 86.3 us -> 77.7 us (0.900)
  starting transfers between devices: 15.9 us -> 11.6 us
  blocking collectives: 16.7 us -> 14.7 us
  waiting for transfers between devices: 10.1 us -> 9.12 us
  Pallas kernels: 40 us -> 39.1 us
    all_to_all x3 -> x2, starting transfers between devices: 15.9 us -> 11 us  [swap(): lax.all_to_all(values, 'box', split_axis=0, concat_axis=0, tiled=True)]
    all_to_all x1, blocking collectives: 16.7 us -> 14.7 us  [swap(): lax.all_to_all(values, 'box', split_axis=0, concat_axis=0, tiled=True)]
    all_to_all x3 -> x2, waiting for transfers between devices: 10.1 us -> 9.11 us  [swap(): lax.all_to_all(values, 'box', split_axis=0, concat_axis=0, tiled=True)]
    pallas_call x5 -> x3, Pallas kernels: 33.1 us -> 32.5 us  [the longest x1 16.6 us: body(): call(functools.partial(far_kernel, blocks, boxes, rcap, cap, slots, kmax,...]
    unnamed x16 -> x8, local copies, waits for them, and re-layouts: 2.01 us -> 1.48 us
  transfers between devices with their start and end apart: 3 -> 4, of which waited for: 2 -> 2; matrix products, arithmetic and copies ran while one was open for 0% -> 0% of each run, Pallas kernels for 36% -> 24%
where the time goes in v3:
time: 77.7 us; the launch traced here: 76.8 us
  Pallas kernels  39.1 us (50%)
  blocking collectives  14.7 us (19%)
  starting transfers between devices  11.6 us (15%)
  waiting for transfers between devices  9.12 us (12%)
  local copies, waits for them, and re-layouts  1.48 us (2%)
    pallas_call x1, Pallas kernels, body(): call(functools.partial(far_kernel, blocks, boxes, rcap, cap, slots, kmax,...  16.6 us
    all_to_all x1, blocking collectives, swap(): lax.all_to_all(values, 'box', split_axis=0, concat_axis=0, tiled=True)  14.7 us
    pallas_call x1, Pallas kernels, body(): call(functools.partial(near_kernel, blocks, boxes, rcap, cap, slots, kmax...  12.9 us
    all_to_all x2, starting transfers between devices, swap(): lax.all_to_all(values, 'box', split_axis=0, concat_axis=0, tiled=True)  11 us
    all_to_all x2, waiting for transfers between devices, swap(): lax.all_to_all(values, 'box', split_axis=0, concat_axis=0, tiled=True)  9.11 us
    pallas_call x1, Pallas kernels, body(): call(functools.partial(plan_kernel, blocks, kmax, rcap, cap, slots, most)...  3 us
    pallas_call x1, Pallas kernels, body(): call(functools.partial(meta_kernel, blocks, boxes, rcap, cap), 'meta', [S...  2.65 us
    pallas_call x1, Pallas kernels, body(): call(functools.partial(answer_kernel, blocks, boxes, rcap), 'answer', [SM...  2.16 us
  transfers between devices with their start and end apart: 4, of which 2 were waited for; matrix products, arithmetic and copies ran while one was open for 0% of the time, Pallas kernels for 24%

profile of v3, /device:TPU:0, one launch (start us, length us, event | category | flops | bytes accessed | tf_op | source)
XLA Modules:
  0.0 76.8 jit_solution(13152201441416513951)
XLA Ops:
  0.6 0.5 collective-permute-start
  1.1 0.1 collective-permute-start.1
  1.2 2.6 %meta.1 = (s32[16,128]{1,0:T(8,128)}, s32[64]{0:T(128)}, s32[64]{0:T(128)}) custom-call(s32[64]{0:T(128)} %move.1, s32[64]{0:T(128)} %age.1, s32[8,16]{1,0:T(8,128)} %bitcast.35), custom_call_target="tpu_custom_call" | custom-call | tf_op jit(solution)/shard_map/meta/pallas_call | solution.py:507
  3.9 7.4 %all-to-all-start = ((s32[16,1,128]{2,1,0:T(1,128)}), s32[16,1,128]{2,1,0:T(1,128)S(1)}, u32[]{:S(2)}, u32[]{:S(2)}) async-start(s32[16,1,128]{2,1,0:T(1,128)} %bitcast.38), calls=%async_computation | async-start | bytes 16384 | tf_op jit(solution)/shard_map/all_to_all | solution.py:459
  11.3 3.0 %plan.1 = (f32[16,96,128]{2,1,0:T(8,128)}, s32[24,128]{1,0:T(8,128)}, s32[40,128]{1,0:T(8,128)}) custom-call(s32[64]{0:T(128)} %get-tuple-element.31.place, f32[64,3,2,128]{3,2,1,0:T(2,128)} %bitcast.31, s32[32,64]{1,0:T(8,128)} %bitcast.37, s32[1,64]{1,0:T(1,128)} %bitcast.40), custom_call_target="tpu_custom_call" | custom-call | tf_op jit(solution)/shard_map/plan/pallas_call | solution.py:517
  14.3 3.3 %all-to-all-done = s32[16,1,128]{2,1,0:T(1,128)S(1)} async-done(((s32[16,1,128]{2,1,0:T(1,128)}), s32[16,1,128]{2,1,0:T(1,128)S(1)}, u32[]{:S(2)}, u32[]{:S(2)}) %all-to-all-start) | async-done | bytes 8224 | tf_op jit(solution)/shard_map/all_to_all | solution.py:459
  17.6 0.0 copy-start.3
  17.6 0.0 collective-permute-done.mate_places
  17.6 0.0 copy-start.1
  17.6 0.0 collective-permute-done.1.mate_gammas
  17.6 0.0 copy-start.2
  17.6 0.6 copy-done.3
  18.2 2.2 %answer.1 = f32[16,96,128]{2,1,0:T(8,128)} custom-call(s32[16,128]{1,0:T(8,128)} %bitcast.33, f32[192,128]{1,0:T(8,128)} %bitcast.25, f32[192,128]{1,0:T(8,128)} %bitcast.29, f32[16,96,128]{2,1,0:T(8,128)} %get-tuple-element.39._), custom_call_target="tpu_custom_call", output_to_operand_aliasing={{}: (3, {})} | custom-call | tf_op jit(solution)/shard_map/answer/pallas_call | solution.py:534
  20.4 0.0 copy-done.1
  20.4 0.0 copy-done.2
  20.4 3.6 %all-to-all-start.1 = ((f32[16,96,128]{2,1,0:T(8,128)}), f32[16,96,128]{2,1,0:T(8,128)S(1)}, u32[]{:S(2)}, u32[]{:S(2)}) async-start(f32[16,96,128]{2,1,0:T(8,128)} %answer.1), calls=%async_computation.1 | async-start | bytes 1572864 | tf_op jit(solution)/shard_map/all_to_all | solution.py:459
  24.0 12.9 %near.1 = (f32[512,128]{1,0:T(8,128)}, bf16[64,32,128]{2,1,0:T(8,128)(2,1)}, f32[8,128]{1,0:T(8,128)}, f32[5,64,128]{2,1,0:T(8,128)}, s32[64]{0:T(128)}, /*index=5*/s32[64]{0:T(128)}) custom-call(s32[24,128]{1,0:T(8,128)} %get-tuple-element.40.plan, s32[40,128]{1,0:T(8,128)} %get-tuple-element.41.ranked, s32[8,16]{1,0:T(8,128)} %bitcast.36, ...), custom_call_target="tpu_custom_call" | custom-call | tf_op jit(solution)/shard_map/near/pallas_call | solution.py:558
  36.9 5.8 %all-to-all-done.1.fetched = f32[16,96,128]{2,1,0:T(8,128)S(1)} async-done(((f32[16,96,128]{2,1,0:T(8,128)}), f32[16,96,128]{2,1,0:T(8,128)S(1)}, u32[]{:S(2)}, u32[]{:S(2)}) %all-to-all-start.1) | async-done | bytes 786464 | tf_op jit(solution)/shard_map/all_to_all | solution.py:459
  42.7 0.0 copy-start
  42.7 0.9 %copy-done = f32[16,96,128]{2,1,0:T(8,128)} copy-done((f32[16,96,128]{2,1,0:T(8,128)}, f32[16,96,128]{2,1,0:T(8,128)S(1)}, u32[]{:S(2)}) %copy-start) | copy-done | bytes 786456
  43.6 16.6 %far.1 = (f32[192,128]{1,0:T(8,128)}, f32[64,3,2,128]{3,2,1,0:T(2,128)}, f32[16,24,128]{2,1,0:T(8,128)}) custom-call(s32[24,128]{1,0:T(8,128)} %get-tuple-element.40.plan, s32[40,128]{1,0:T(8,128)} %get-tuple-element.41.ranked, s32[64]{0:T(128)} %get-tuple-element.44.moved_from, s32[64]{0:T(128)} %get-tuple-element.45.age_place, f32[16,96,128]{2,1,0:T(8,128)} %copy-done, ...), custom_call_target="tpu_custom_call" | custom-call | tf_op jit(solution)/shard_map/far/pallas_call | solution.py:576
  60.2 14.7 %all_to_all.22.arrived = f32[16,24,128]{2,1,0:T(8,128)} all-to-all(f32[16,24,128]{2,1,0:T(8,128)} %get-tuple-element.55), channel_id=1, replica_groups=mesh['cases'=2,'box'=16] {'box'}, dimensions={0} | all-to-all | bytes 393216 | tf_op jit(solution)/shard_map/all_to_all | solution.py:459
  74.9 1.9 %frame.1 = f32[192,128]{1,0:T(8,128)} custom-call(s32[64]{0:T(128)} %get-tuple-element.54.aged_from, f32[16,24,128]{2,1,0:T(8,128)} %all_to_all.22.arrived, f32[5,64,128]{2,1,0:T(8,128)} %get-tuple-element.56.tables), custom_call_target="tpu_custom_call" | custom-call | tf_op jit(solution)/shard_map/frame/pallas_call | solution.py:588
Async XLA Ops:
  0.6 17.0 %collective-permute-start = (f32[192,128]{1,0:T(8,128)}, f32[192,128]{1,0:T(8,128)S(1)}, u32[]{:S(2)}, u32[]{:S(2)}) collective-permute-start(f32[192,128]{1,0:T(8,128)} %bitcast.24), channel_id=1, source_target_pairs={{0,1},{1,0},{2,3},{3,2},{4,5},{5,4},{6,7},{7,6},{8,9},{9,8},{10,11... | collective-permute-start | bytes 294920 | tf_op jit(solution)/shard_map/ppermute | solution.py:529
  1.1 16.5 %collective-permute-start.1 = (f32[192,128]{1,0:T(8,128)}, f32[192,128]{1,0:T(8,128)S(1)}, u32[]{:S(2)}, u32[]{:S(2)}) collective-permute-start(f32[192,128]{1,0:T(8,128)} %bitcast.28), channel_id=1, source_target_pairs={{0,1},{1,0},{2,3},{3,2},{4,5},{5,4},{6,7},{7,6},{8,9},{9,8},{10,11... | collective-permute-start | bytes 294920 | tf_op jit(solution)/shard_map/ppermute | solution.py:530
  3.9 13.7 %all-to-all-start = ((s32[16,1,128]{2,1,0:T(1,128)}), s32[16,1,128]{2,1,0:T(1,128)S(1)}, u32[]{:S(2)}, u32[]{:S(2)}) async-start(s32[16,1,128]{2,1,0:T(1,128)} %bitcast.38), calls=%async_computation | async-start | bytes 16384 | tf_op jit(solution)/shard_map/all_to_all | solution.py:459
  17.6 0.6 copy-start.3
  17.6 2.8 %copy-start.1 = (f32[192,128]{1,0:T(8,128)}, f32[192,128]{1,0:T(8,128)S(1)}, u32[]{:S(2)}) copy-start(f32[192,128]{1,0:T(8,128)S(1)} %collective-permute-done.mate_places) | copy-start | bytes 294916
  17.6 2.8 %copy-start.2 = (f32[192,128]{1,0:T(8,128)}, f32[192,128]{1,0:T(8,128)S(1)}, u32[]{:S(2)}) copy-start(f32[192,128]{1,0:T(8,128)S(1)} %collective-permute-done.1.mate_gammas) | copy-start | bytes 294916
  20.4 22.3 %all-to-all-start.1 = ((f32[16,96,128]{2,1,0:T(8,128)}), f32[16,96,128]{2,1,0:T(8,128)S(1)}, u32[]{:S(2)}, u32[]{:S(2)}) async-start(f32[16,96,128]{2,1,0:T(8,128)} %answer.1), calls=%async_computation.1 | async-start | bytes 1572864 | tf_op jit(solution)/shard_map/all_to_all | solution.py:459
  42.7 0.9 %copy-start = (f32[16,96,128]{2,1,0:T(8,128)}, f32[16,96,128]{2,1,0:T(8,128)S(1)}, u32[]{:S(2)}) copy-start(f32[16,96,128]{2,1,0:T(8,128)S(1)} %all-to-all-done.1.fetched) | copy-start | bytes 2359300

commit v4 on v3

--- a/solution.py
+++ b/solution.py
@@ -16,7 +16,7 @@
 
 LANES = 128
 FEATURES = 32
-UNROLL = 32
+UNROLL = 48
 BUILD = 8
 BF = jnp.bfloat16
 F32 = jnp.float32
@@ -38,37 +38,30 @@
     return lax.broadcasted_iota(I32, dims, axis)
 
 
-def meta_kernel(blocks, boxes, rcap, cap, move, age, fetch, meta, move_place, age_place, fill):
-    def ask(p, carry):
-        for lane in range(rcap):
-            meta[p, lane] = fetch[lane, p]
-        fill[p] = 0
-        fill[boxes + p] = 0
-        return carry
-
-    lax.fori_loop(0, boxes, ask, 0, unroll=4)
-
-    def place(g, carry):
-        for source, first, target, lane in (
-            (move, 0, move_place, rcap),
-            (age, boxes, age_place, rcap + cap),
-        ):
-            block = source[g]
-            box = lax.div(block, blocks)
-            rank = fill[first + box]
-            fill[first + box] = rank + 1
-            meta[box, lane + rank] = block - box * blocks
-            target[g] = box * 256 + rank
-        return carry
-
-    lax.fori_loop(0, blocks, place, 0, unroll=4)
-
-    def number(p, carry):
-        meta[p, rcap + 2 * cap] = fill[p]
-        meta[p, rcap + 2 * cap + 1] = fill[boxes + p]
-        return carry
-
-    lax.fori_loop(0, boxes, number, 0, unroll=4)
+def meta_kernel(blocks, boxes, rcap, cap, move, age, fetch, meta):
+    def product(left, right, contract=1):
+        return lax.dot_general(
+            left.astype(BF), right.astype(BF), (((1,), (contract,)), ((), ())),
+            preferred_element_type=F32,
+        )
+
+    def flag(condition):
+        return jnp.where(condition, 1.0, 0.0)
+
+    asked = product(flag(iota((boxes, boxes), 0) == iota((boxes, boxes), 1)), fetch[...].astype(F32), 1)
+    row = product(asked, flag(iota((rcap, LANES), 0) == iota((rcap, LANES), 1)), 0)
+    before = flag(iota((blocks, blocks), 0) < iota((blocks, blocks), 1))
+    diagonal = iota((blocks, blocks), 0) == iota((blocks, blocks), 1)
+    lane = iota((blocks, LANES), 1)
+    for n, source in enumerate((move, age)):
+        block = source[...]
+        sent = flag(lax.div(block, blocks) == iota((boxes, blocks), 0))
+        rank = jnp.sum(sent * product(sent, before, 0), axis=0, keepdims=True)
+        turned = product(jnp.where(diagonal, rank, 0.0), jnp.ones((blocks, LANES), F32), 0)
+        place = flag(turned.astype(I32) + (rcap + n * cap) == lane)
+        row = row + product(sent * lax.rem(block, blocks).astype(F32), place, 0)
+        row = row + product(sent, flag(lane == rcap + 2 * cap + n), 0)
+    meta[...] = row.astype(I32)
 
 
 def plan_rows(slots, most):
@@ -77,12 +70,26 @@
     return chunks, users, (2 * chunks + users + 3 + 7) // 8 * 8
 
 
-def plan_kernel(blocks, kmax, rcap, cap, slots, most, place, history, tiles, count,
-                message, plan, ranked, packed, sem):
+def plan_kernel(blocks, boxes, kmax, rcap, cap, slots, most, move, age, history, tiles, count,
+                message, plan, ranked, age_place, packed, filled, sem):
+    def clear(p, carry):
+        filled[p] = 0
+        return carry
+
+    lax.fori_loop(0, 2 * boxes, clear, 0, unroll=8)
+    shift = blocks.bit_length() - 1
+
+    def owner(block):
+        return block >> shift if 1 << shift == blocks else lax.div(block, blocks)
+
     def one(g, carry):
-        where = place[g]
-        box = where >> 8
-        rank = where & 255
+        box = owner(age[g])
+        rank = filled[boxes + box]
+        filled[boxes + box] = rank + 1
+        age_place[g] = box * 256 + rank
+        box = owner(move[g])
+        rank = filled[box]
+        filled[box] = rank + 1
         for axis in range(3):
             packed[box, pl.ds(axis * cap + rank, 2, stride=3 * cap), :] = history[g, axis]
         return carry
@@ -130,7 +137,7 @@
             row = part * chunks + chunk
             plan[row : row + 1, :] = word
         row = rows - 3 + part
-        plan[row : row + 1, :] = (stop - begin + (UNROLL - 1)) >> (UNROLL.bit_length() - 1)
+        plan[row : row + 1, :] = lax.div(stop - begin + (UNROLL - 1), UNROLL)
         if part == 0:
             begin = stop
             behind = tally[last - 1 : last, :]
@@ -459,7 +466,7 @@
     return lax.all_to_all(values, "box", split_axis=0, concat_axis=0, tiled=True)
 
 
-def call(kernel, name, in_specs, outs, scratch=(), aliases={}):
+def call(kernel, name, in_specs, outs, scratch=(), aliases={}, limit=65400 << 10):
     several = isinstance(outs, list)
     listed = outs if several else [outs]
     specs = [spec for spec, _, _ in listed]
@@ -471,7 +478,7 @@
         out_shape=shapes if several else shapes[0],
         scratch_shapes=list(scratch),
         input_output_aliases=aliases,
-        compiler_params=pltpu.CompilerParams(vmem_limit_bytes=60 << 20),
+        compiler_params=pltpu.CompilerParams(vmem_limit_bytes=limit),
         name=name,
     )
 
@@ -504,33 +511,36 @@
     past = jnp.transpose(history, (0, 2, 1, 3))
 
     asked = fetch_list[0].T
-    meta, move_place, age_place = call(
+    meta = call(
         functools.partial(meta_kernel, blocks, boxes, rcap, cap),
         "meta",
-        [SMEM] * 3,
-        [(SMEM, (boxes, LANES), I32), (SMEM, (blocks,), I32), (SMEM, (blocks,), I32)],
-        [pltpu.SMEM((2 * boxes,), I32)],
-    )(move_list, age_slot, asked)
+        [VMEM] * 3,
+        (VMEM, (boxes, LANES), I32),
+    )(move_list.reshape(1, blocks), age_slot.reshape(1, blocks), asked)
     labels = swap(meta)
     past_rows = (6 * cap + 7) // 8 * 8
     message_shape = (boxes, 6 * rcap + past_rows, LANES)
-    message, plan, ranked = call(
-        functools.partial(plan_kernel, blocks, kmax, rcap, cap, slots, most),
+    message, plan, ranked, age_place = call(
+        functools.partial(plan_kernel, blocks, boxes, kmax, rcap, cap, slots, most),
         "plan",
-        [SMEM] + [VMEM] * 3,
+        [SMEM] * 2 + [VMEM] * 3,
         [
             (ANY, message_shape, F32),
             (VMEM, (rows, LANES), I32),
             (VMEM, (groups * (kmax + 8), LANES), I32),
+            (SMEM, (blocks,), I32),
         ],
-        [pltpu.VMEM((boxes, past_rows, LANES), F32), pltpu.SemaphoreType.DMA],
-    )(move_place, past, tile_slot.T, tile_count.reshape(1, blocks))
+        [
+            pltpu.VMEM((boxes, past_rows, LANES), F32),
+            pltpu.SMEM((2 * boxes,), I32),
+            pltpu.SemaphoreType.DMA,
+        ],
+    )(move_list, age_slot, past, tile_slot.T, tile_count.reshape(1, blocks))
     mates = [(box, box ^ 1) for box in range(boxes)]
-    mate_places = lax.ppermute(places, "box", mates)
-    mate_gammas = lax.ppermute(gammas, "box", mates)
-    labels, message, plan, ranked, mate_places, mate_gammas = lax.optimization_barrier(
-        (labels, message, plan, ranked, mate_places, mate_gammas)
-    )
+    own_places, own_gammas, plan = lax.optimization_barrier((places, gammas, plan))
+    mate_places = lax.ppermute(own_places, "box", mates)
+    mate_gammas = lax.ppermute(own_gammas, "box", mates)
+    labels, message, plan, ranked = lax.optimization_barrier((labels, message, plan, ranked))
     message = call(
         functools.partial(answer_kernel, blocks, boxes, rcap),
         "answer",
@@ -538,10 +548,9 @@
         (ANY, message_shape, F32),
         [pltpu.VMEM((boxes, 6 * rcap, LANES), F32), pltpu.SemaphoreType.DMA((4,))],
         {3: 0},
+        limit=65400 << 10,
     )(labels, places, gammas, message)
-    plan, ranked, mate_places, message = lax.optimization_barrier(
-        (plan, ranked, mate_places, message)
-    )
+    plan, ranked, message = lax.optimization_barrier((plan, ranked, message))
     fetched = swap(message)
 
     def scratch(owners):
@@ -583,6 +592,7 @@
             (VMEM, (boxes, 3 * cap, LANES), F32),
         ],
         [pltpu.VMEM((3 * blocks, LANES), F32)] + scratch(boxes),
+        limit=65400 << 10,
     )(plan, ranked, moved_from, age_place, fetched, places, targets, centre, partial)
     aged = swap(outgoing)
     frame = call(
@@ -590,6 +600,7 @@
         "frame",
         [SMEM, VMEM, VMEM],
         (VMEM, (3 * blocks, LANES), F32),
+        limit=65400 << 10,
     )(aged_from, aged, turns)
 
     def back(rows):

time: 77.7 us -> 76.6 us (0.986)
  blocking collectives: 14.7 us -> 16.5 us
  waiting for transfers between devices: 9.12 us -> 7.48 us
  Pallas kernels: 39.1 us -> 37.7 us
  starting transfers between devices: 11.6 us -> 12.4 us
    all_to_all x2, waiting for transfers between devices: 9.11 us -> 6.46 us  [swap(): lax.all_to_all(values, 'box', split_axis=0, concat_axis=0, tiled=True)]
    all_to_all x1, blocking collectives: 14.7 us -> 16.5 us  [swap(): lax.all_to_all(values, 'box', split_axis=0, concat_axis=0, tiled=True)]
    ppermute x2, waiting for transfers between devices: 0.01 us -> 1.02 us  [the longest x1 0.79 us: body(): mate_places = lax.ppermute(own_places, 'box', mates)]
    all_to_all x2, starting transfers between devices: 11 us -> 11.8 us  [swap(): lax.all_to_all(values, 'box', split_axis=0, concat_axis=0, tiled=True)]
    unnamed x8 -> x10, local copies, waits for them, and re-layouts: 1.48 us -> 1.66 us
  transfers between devices with their start and end apart: 4 -> 4, of which waited for: 2 -> 4; matrix products, arithmetic and copies ran while one was open for 0% -> 0% of each run, Pallas kernels for 24% -> 21%
where the time goes in v4:
time: 76.6 us; the launch traced here: 76.5 us
  Pallas kernels  37.7 us (49%)
  blocking collectives  16.5 us (22%)
  starting transfers between devices  12.4 us (16%)
  waiting for transfers between devices  7.48 us (10%)
  local copies, waits for them, and re-layouts  1.66 us (2%)
    all_to_all x1, blocking collectives, swap(): lax.all_to_all(values, 'box', split_axis=0, concat_axis=0, tiled=True)  16.5 us
    pallas_call x1, Pallas kernels, body(): call(functools.partial(far_kernel, blocks, boxes, rcap, cap, slots, kmax,...  15.9 us
    pallas_call x1, Pallas kernels, body(): call(functools.partial(near_kernel, blocks, boxes, rcap, cap, slots, kmax...  12.4 us
    all_to_all x2, starting transfers between devices, swap(): lax.all_to_all(values, 'box', split_axis=0, concat_axis=0, tiled=True)  11.8 us
    all_to_all x2, waiting for transfers between devices, swap(): lax.all_to_all(values, 'box', split_axis=0, concat_axis=0, tiled=True)  6.46 us
    pallas_call x1, Pallas kernels, body(): call(functools.partial(plan_kernel, blocks, boxes, kmax, rcap, cap, slots...  3.48 us
    pallas_call x1, Pallas kernels, body(): call(functools.partial(answer_kernel, blocks, boxes, rcap), 'answer', [SM...  2.18 us
    pallas_call x1, Pallas kernels, body(): call(functools.partial(frame_kernel, blocks, cap), 'frame', [SMEM, VMEM,...  1.88 us
  transfers between devices with their start and end apart: 4, of which 4 were waited for; matrix products, arithmetic and copies ran while one was open for 0% of the time, Pallas kernels for 21%

profile of v4, /device:TPU:0, one launch (start us, length us, event | category | flops | bytes accessed | tf_op | source)
XLA Modules:
  0.0 76.5 jit_solution(12418698752539320026)
XLA Ops:
  0.6 1.8 %meta.1 = s32[16,128]{1,0:T(8,128)} custom-call(s32[1,64]{1,0:T(1,128)} %bitcast.42, s32[1,64]{1,0:T(1,128)} %bitcast.43, s32[8,16]{1,0:T(8,128)} %bitcast.38), custom_call_target="tpu_custom_call" | custom-call | tf_op jit(solution)/shard_map/meta/pallas_call | solution.py:514
  2.5 7.4 %all-to-all-start = ((s32[16,1,128]{2,1,0:T(1,128)}), s32[16,1,128]{2,1,0:T(1,128)S(1)}, u32[]{:S(2)}, u32[]{:S(2)}) async-start(s32[16,1,128]{2,1,0:T(1,128)} %bitcast.37), calls=%async_computation | async-start | bytes 16384 | tf_op jit(solution)/shard_map/all_to_all | solution.py:466
  9.9 3.5 %plan.1 = (f32[16,96,128]{2,1,0:T(8,128)}, s32[24,128]{1,0:T(8,128)}, s32[40,128]{1,0:T(8,128)}, s32[64]{0:T(128)}) custom-call(s32[64]{0:T(128)} %move.1, s32[64]{0:T(128)} %age.1, f32[64,3,2,128]{3,2,1,0:T(2,128)} %bitcast.33, s32[32,64]{1,0:T(8,128)} %bitcast.40, s32[1,64]{1,0:T(1,128)} %bitcast.44), custom_call_target="tpu_custom_call" | custom-call | tf_op jit(solution)/shard_map/plan/pallas_call | solution.py:523
  13.3 2.8 %all-to-all-done = s32[16,1,128]{2,1,0:T(1,128)S(1)} async-done(((s32[16,1,128]{2,1,0:T(1,128)}), s32[16,1,128]{2,1,0:T(1,128)S(1)}, u32[]{:S(2)}, u32[]{:S(2)}) %all-to-all-start) | async-done | bytes 8224 | tf_op jit(solution)/shard_map/all_to_all | solution.py:466
  16.2 0.0 copy-start.4
  16.2 0.6 copy-done.4
  16.8 2.2 %answer.1 = f32[16,96,128]{2,1,0:T(8,128)} custom-call(s32[16,128]{1,0:T(8,128)} %bitcast.35, f32[192,128]{1,0:T(8,128)} %bitcast.26, f32[192,128]{1,0:T(8,128)} %bitcast.30, f32[16,96,128]{2,1,0:T(8,128)} %get-tuple-element.35._), custom_call_target="tpu_custom_call", output_to_operand_aliasing={{}: (3, {})} | custom-call | tf_op jit(solution)/shard_map/answer/pallas_call | solution.py:544
  19.0 0.0 copy-start
  19.0 0.0 copy-start.1
  19.0 4.4 %all-to-all-start.1 = ((f32[16,96,128]{2,1,0:T(8,128)}), f32[16,96,128]{2,1,0:T(8,128)}, u32[]{:S(2)}, u32[]{:S(2)}) async-start(f32[16,96,128]{2,1,0:T(8,128)} %answer.1), calls=%async_computation.1 | async-start | bytes 1572864 | tf_op jit(solution)/shard_map/all_to_all | solution.py:466
  23.4 0.0 copy-done
  23.5 0.3 collective-permute-start
  23.8 0.0 copy-done.1
  23.8 0.3 collective-permute-start.1
  24.0 0.8 %collective-permute-done.mate_places = f32[192,128]{1,0:T(8,128)S(1)} collective-permute-done((f32[192,128]{1,0:T(8,128)S(1)}, f32[192,128]{1,0:T(8,128)S(1)}, u32[]{:S(2)}, u32[]{:S(2)}) %collective-permute-start) | collective-permute-done | bytes 98336 | tf_op jit(solution)/shard_map/ppermute | solution.py:541
  24.8 0.0 copy-start.2
  24.8 0.2 collective-permute-done.1.mate_gammas
  25.1 0.4 copy-done.2
  25.5 0.0 copy-start.3
  25.5 0.6 copy-done.3
  26.1 12.4 %near.1 = (f32[512,128]{1,0:T(8,128)}, bf16[64,32,128]{2,1,0:T(8,128)(2,1)}, f32[8,128]{1,0:T(8,128)}, f32[5,64,128]{2,1,0:T(8,128)}, s32[64]{0:T(128)}, /*index=5*/s32[64]{0:T(128)}) custom-call(s32[24,128]{1,0:T(8,128)} %get-tuple-element.36.plan, s32[40,128]{1,0:T(8,128)} %get-tuple-element.37.ranked, s32[8,16]{1,0:T(8,128)} %bitcast.39, ...), custom_call_target="tpu_custom_call" | custom-call | tf_op jit(solution)/shard_map/near/pallas_call | solution.py:567
  38.5 3.6 %all-to-all-done.1.fetched = f32[16,96,128]{2,1,0:T(8,128)} async-done(((f32[16,96,128]{2,1,0:T(8,128)}), f32[16,96,128]{2,1,0:T(8,128)}, u32[]{:S(2)}, u32[]{:S(2)}) %all-to-all-start.1) | async-done | bytes 786464 | tf_op jit(solution)/shard_map/all_to_all | solution.py:466
  42.2 15.9 %far.1 = (f32[192,128]{1,0:T(8,128)}, f32[64,3,2,128]{3,2,1,0:T(2,128)}, f32[16,24,128]{2,1,0:T(8,128)}) custom-call(s32[24,128]{1,0:T(8,128)} %get-tuple-element.36.plan, s32[40,128]{1,0:T(8,128)} %get-tuple-element.37.ranked, s32[64]{0:T(128)} %get-tuple-element.40.moved_from, s32[64]{0:T(128)} %get-tuple-element.41.age_place, ...), custom_call_target="tpu_custom_call" | custom-call | tf_op jit(solution)/shard_map/far/pallas_call | solution.py:585
  58.1 16.5 %all_to_all.22.arrived = f32[16,24,128]{2,1,0:T(8,128)} all-to-all(f32[16,24,128]{2,1,0:T(8,128)} %get-tuple-element.51), channel_id=1, replica_groups=mesh['cases'=2,'box'=16] {'box'}, dimensions={0} | all-to-all | bytes 393216 | tf_op jit(solution)/shard_map/all_to_all | solution.py:466
  74.6 1.9 %frame.1 = f32[192,128]{1,0:T(8,128)} custom-call(s32[64]{0:T(128)} %get-tuple-element.50.aged_from, f32[16,24,128]{2,1,0:T(8,128)} %all_to_all.22.arrived, f32[5,64,128]{2,1,0:T(8,128)} %get-tuple-element.52.tables), custom_call_target="tpu_custom_call" | custom-call | tf_op jit(solution)/shard_map/frame/pallas_call | solution.py:598
Async XLA Ops:
  2.5 13.7 %all-to-all-start = ((s32[16,1,128]{2,1,0:T(1,128)}), s32[16,1,128]{2,1,0:T(1,128)S(1)}, u32[]{:S(2)}, u32[]{:S(2)}) async-start(s32[16,1,128]{2,1,0:T(1,128)} %bitcast.37), calls=%async_computation | async-start | bytes 16384 | tf_op jit(solution)/shard_map/all_to_all | solution.py:466
  16.2 0.6 copy-start.4
  19.0 4.5 %copy-start = (f32[64,3,128]{2,0,1:T(8,128)S(1)}, f32[64,3,128]{2,0,1:T(8,128)}, u32[]{:S(2)}) copy-start(f32[64,3,128]{2,0,1:T(8,128)} %param.11) | copy-start | bytes 294916
  19.0 4.8 %copy-start.1 = (f32[64,3,128]{2,0,1:T(8,128)S(1)}, f32[64,3,128]{2,0,1:T(8,128)}, u32[]{:S(2)}) copy-start(f32[64,3,128]{2,0,1:T(8,128)} %param.12) | copy-start | bytes 294916
  19.0 23.2 %all-to-all-start.1 = ((f32[16,96,128]{2,1,0:T(8,128)}), f32[16,96,128]{2,1,0:T(8,128)}, u32[]{:S(2)}, u32[]{:S(2)}) async-start(f32[16,96,128]{2,1,0:T(8,128)} %answer.1), calls=%async_computation.1 | async-start | bytes 1572864 | tf_op jit(solution)/shard_map/all_to_all | solution.py:466
  23.5 1.4 %collective-permute-start = (f32[192,128]{1,0:T(8,128)S(1)}, f32[192,128]{1,0:T(8,128)S(1)}, u32[]{:S(2)}, u32[]{:S(2)}) collective-permute-start(f32[192,128]{1,0:T(8,128)S(1)} %bitcast.29), channel_id=1, source_target_pairs={{0,1},{1,0},{2,3},{3,2},{4,5},{5,4},{6,7},{7,6},{8,9},{9,8},{10,11... | collective-permute-start | bytes 294920 | tf_op jit(solution)/shard_map/ppermute | solution.py:541
  23.8 1.3 %collective-permute-start.1 = (f32[192,128]{1,0:T(8,128)S(1)}, f32[192,128]{1,0:T(8,128)S(1)}, u32[]{:S(2)}, u32[]{:S(2)}) collective-permute-start(f32[192,128]{1,0:T(8,128)S(1)} %bitcast.32), channel_id=1, source_target_pairs={{0,1},{1,0},{2,3},{3,2},{4,5},{5,4},{6,7},{7,6},{8,9},{9,8},{10,11... | collective-permute-start | bytes 294920 | tf_op jit(solution)/shard_map/ppermute | solution.py:542
  24.8 0.6 copy-start.2
  25.5 0.6 copy-start.3

commit v5 on v4

--- a/solution.py
+++ b/solution.py
@@ -17,7 +17,7 @@
 LANES = 128
 FEATURES = 32
 UNROLL = 48
-BUILD = 8
+BUILD = 16
 BF = jnp.bfloat16
 F32 = jnp.float32
 I32 = jnp.int32
@@ -228,7 +228,7 @@
                 ]
             return carry
 
-        lax.fori_loop(first, first + quarter, one, 0)
+        lax.fori_loop(first, first + quarter, one, 0, unroll=4)
         peers = pl.ds(first, quarter)
         copy = pltpu.make_async_copy(
             packed.at[peers], message.at[peers, pl.ds(0, 6 * rcap), :], sems.at[part]
@@ -466,7 +466,7 @@
     return lax.all_to_all(values, "box", split_axis=0, concat_axis=0, tiled=True)
 
 
-def call(kernel, name, in_specs, outs, scratch=(), aliases={}, limit=65400 << 10):
+def call(kernel, name, in_specs, outs, scratch=(), aliases={}, limit=64 << 20):
     several = isinstance(outs, list)
     listed = outs if several else [outs]
     specs = [spec for spec, _, _ in listed]

time: 76.6 us -> 75.7 us (0.988)
    unnamed x10 -> x8, local copies, waits for them, and re-layouts: 1.66 us -> 1.06 us
where the time goes in v5:
time: 75.7 us; the launch traced here: 75.9 us
  Pallas kernels  37.1 us (49%)
  blocking collectives  17.1 us (23%)
  starting transfers between devices  12.4 us (16%)
  waiting for transfers between devices  7.53 us (10%)
  local copies, waits for them, and re-layouts  1.06 us (1%)
    all_to_all x1, blocking collectives, swap(): lax.all_to_all(values, 'box', split_axis=0, concat_axis=0, tiled=True)  17.1 us
    pallas_call x1, Pallas kernels, body(): call(functools.partial(far_kernel, blocks, boxes, rcap, cap, slots, kmax,...  15.4 us
    pallas_call x1, Pallas kernels, body(): call(functools.partial(near_kernel, blocks, boxes, rcap, cap, slots, kmax...  12.4 us
    all_to_all x2, starting transfers between devices, swap(): lax.all_to_all(values, 'box', split_axis=0, concat_axis=0, tiled=True)  11.9 us
    all_to_all x2, waiting for transfers between devices, swap(): lax.all_to_all(values, 'box', split_axis=0, concat_axis=0, tiled=True)  6.51 us
    pallas_call x1, Pallas kernels, body(): call(functools.partial(plan_kernel, blocks, boxes, kmax, rcap, cap, slots...  3.48 us
    pallas_call x1, Pallas kernels, body(): call(functools.partial(answer_kernel, blocks, boxes, rcap), 'answer', [SM...  2.04 us
    pallas_call x1, Pallas kernels, body(): call(functools.partial(frame_kernel, blocks, cap), 'frame', [SMEM, VMEM,...  1.88 us
  transfers between devices with their start and end apart: 4, of which 4 were waited for; matrix products, arithmetic and copies ran while one was open for 0% of the time, Pallas kernels for 21%

profile of v5, /device:TPU:0, one launch (start us, length us, event | category | flops | bytes accessed | tf_op | source)
XLA Modules:
  0.0 75.9 jit_solution(6599113653929576292)
XLA Ops:
  0.6 1.8 %meta.1 = s32[16,128]{1,0:T(8,128)} custom-call(s32[1,64]{1,0:T(1,128)} %bitcast.40, s32[1,64]{1,0:T(1,128)} %bitcast.41, s32[8,16]{1,0:T(8,128)} %bitcast.36), custom_call_target="tpu_custom_call" | custom-call | tf_op jit(solution)/shard_map/meta/pallas_call | solution.py:514
  2.5 7.4 %all-to-all-start = ((s32[16,1,128]{2,1,0:T(1,128)}), s32[16,1,128]{2,1,0:T(1,128)}, u32[]{:S(2)}, u32[]{:S(2)}) async-start(s32[16,1,128]{2,1,0:T(1,128)} %bitcast.35), calls=%async_computation | async-start | bytes 16384 | tf_op jit(solution)/shard_map/all_to_all | solution.py:466
  9.9 3.5 %plan.1 = (f32[16,96,128]{2,1,0:T(8,128)}, s32[24,128]{1,0:T(8,128)}, s32[40,128]{1,0:T(8,128)}, s32[64]{0:T(128)}) custom-call(s32[64]{0:T(128)} %move.1, s32[64]{0:T(128)} %age.1, f32[64,3,2,128]{3,2,1,0:T(2,128)} %bitcast.33, s32[32,64]{1,0:T(8,128)} %bitcast.38, s32[1,64]{1,0:T(1,128)} %bitcast.42), custom_call_target="tpu_custom_call" | custom-call | tf_op jit(solution)/shard_map/plan/pallas_call | solution.py:523
  13.4 2.9 %all-to-all-done = s32[16,1,128]{2,1,0:T(1,128)} async-done(((s32[16,1,128]{2,1,0:T(1,128)}), s32[16,1,128]{2,1,0:T(1,128)}, u32[]{:S(2)}, u32[]{:S(2)}) %all-to-all-start) | async-done | bytes 8224 | tf_op jit(solution)/shard_map/all_to_all | solution.py:466
  16.3 2.0 %answer.1 = f32[16,96,128]{2,1,0:T(8,128)} custom-call(s32[16,128]{1,0:T(8,128)} %bitcast.6.asked.labels, f32[192,128]{1,0:T(8,128)} %bitcast.26, f32[192,128]{1,0:T(8,128)} %bitcast.30, f32[16,96,128]{2,1,0:T(8,128)} %get-tuple-element.35._), custom_call_target="tpu_custom_call", output_to_operand_aliasing={{}: (3, {})} | custom-call | tf_op jit(solution)/shard_map/answer/pallas_call | solution.py:544
  18.3 0.0 copy-start
  18.4 0.0 copy-start.1
  18.4 4.4 %all-to-all-start.1 = ((f32[16,96,128]{2,1,0:T(8,128)}), f32[16,96,128]{2,1,0:T(8,128)}, u32[]{:S(2)}, u32[]{:S(2)}) async-start(f32[16,96,128]{2,1,0:T(8,128)} %answer.1), calls=%async_computation.1 | async-start | bytes 1572864 | tf_op jit(solution)/shard_map/all_to_all | solution.py:466
  22.8 0.0 copy-done
  22.8 0.3 collective-permute-start
  23.1 0.0 copy-done.1
  23.1 0.3 collective-permute-start.1
  23.4 0.8 %collective-permute-done.mate_places = f32[192,128]{1,0:T(8,128)S(1)} collective-permute-done((f32[192,128]{1,0:T(8,128)S(1)}, f32[192,128]{1,0:T(8,128)S(1)}, u32[]{:S(2)}, u32[]{:S(2)}) %collective-permute-start) | collective-permute-done | bytes 98336 | tf_op jit(solution)/shard_map/ppermute | solution.py:541
  24.2 0.0 copy-start.2
  24.2 0.2 collective-permute-done.1.mate_gammas
  24.4 0.4 copy-done.2
  24.8 0.0 copy-start.3
  24.8 0.6 copy-done.3
  25.5 12.4 %near.1 = (f32[512,128]{1,0:T(8,128)}, bf16[64,32,128]{2,1,0:T(8,128)(2,1)}, f32[8,128]{1,0:T(8,128)}, f32[5,64,128]{2,1,0:T(8,128)}, s32[64]{0:T(128)}, /*index=5*/s32[64]{0:T(128)}) custom-call(s32[24,128]{1,0:T(8,128)} %get-tuple-element.36.plan, s32[40,128]{1,0:T(8,128)} %get-tuple-element.37.ranked, s32[8,16]{1,0:T(8,128)} %bitcast.37, ...), custom_call_target="tpu_custom_call" | custom-call | tf_op jit(solution)/shard_map/near/pallas_call | solution.py:567
  37.9 3.6 %all-to-all-done.1.fetched = f32[16,96,128]{2,1,0:T(8,128)} async-done(((f32[16,96,128]{2,1,0:T(8,128)}), f32[16,96,128]{2,1,0:T(8,128)}, u32[]{:S(2)}, u32[]{:S(2)}) %all-to-all-start.1) | async-done | bytes 786464 | tf_op jit(solution)/shard_map/all_to_all | solution.py:466
  41.5 15.4 %far.1 = (f32[192,128]{1,0:T(8,128)}, f32[64,3,2,128]{3,2,1,0:T(2,128)}, f32[16,24,128]{2,1,0:T(8,128)}) custom-call(s32[24,128]{1,0:T(8,128)} %get-tuple-element.36.plan, s32[40,128]{1,0:T(8,128)} %get-tuple-element.37.ranked, s32[64]{0:T(128)} %get-tuple-element.40.moved_from, s32[64]{0:T(128)} %get-tuple-element.41.age_place, ...), custom_call_target="tpu_custom_call" | custom-call | tf_op jit(solution)/shard_map/far/pallas_call | solution.py:585
  57.0 17.1 %all_to_all.22.arrived = f32[16,24,128]{2,1,0:T(8,128)} all-to-all(f32[16,24,128]{2,1,0:T(8,128)} %get-tuple-element.51), channel_id=1, replica_groups=mesh['cases'=2,'box'=16] {'box'}, dimensions={0} | all-to-all | bytes 393216 | tf_op jit(solution)/shard_map/all_to_all | solution.py:466
  74.1 1.9 %frame.1 = f32[192,128]{1,0:T(8,128)} custom-call(s32[64]{0:T(128)} %get-tuple-element.50.aged_from, f32[16,24,128]{2,1,0:T(8,128)} %all_to_all.22.arrived, f32[5,64,128]{2,1,0:T(8,128)} %get-tuple-element.52.tables), custom_call_target="tpu_custom_call" | custom-call | tf_op jit(solution)/shard_map/frame/pallas_call | solution.py:598
Async XLA Ops:
  2.5 13.8 %all-to-all-start = ((s32[16,1,128]{2,1,0:T(1,128)}), s32[16,1,128]{2,1,0:T(1,128)}, u32[]{:S(2)}, u32[]{:S(2)}) async-start(s32[16,1,128]{2,1,0:T(1,128)} %bitcast.35), calls=%async_computation | async-start | bytes 16384 | tf_op jit(solution)/shard_map/all_to_all | solution.py:466
  18.3 4.5 %copy-start = (f32[64,3,128]{2,0,1:T(8,128)S(1)}, f32[64,3,128]{2,0,1:T(8,128)}, u32[]{:S(2)}) copy-start(f32[64,3,128]{2,0,1:T(8,128)} %param.11) | copy-start | bytes 294916
  18.4 4.8 %copy-start.1 = (f32[64,3,128]{2,0,1:T(8,128)S(1)}, f32[64,3,128]{2,0,1:T(8,128)}, u32[]{:S(2)}) copy-start(f32[64,3,128]{2,0,1:T(8,128)} %param.12) | copy-start | bytes 294916
  18.4 23.1 %all-to-all-start.1 = ((f32[16,96,128]{2,1,0:T(8,128)}), f32[16,96,128]{2,1,0:T(8,128)}, u32[]{:S(2)}, u32[]{:S(2)}) async-start(f32[16,96,128]{2,1,0:T(8,128)} %answer.1), calls=%async_computation.1 | async-start | bytes 1572864 | tf_op jit(solution)/shard_map/all_to_all | solution.py:466
  22.8 1.4 %collective-permute-start = (f32[192,128]{1,0:T(8,128)S(1)}, f32[192,128]{1,0:T(8,128)S(1)}, u32[]{:S(2)}, u32[]{:S(2)}) collective-permute-start(f32[192,128]{1,0:T(8,128)S(1)} %bitcast.29), channel_id=1, source_target_pairs={{0,1},{1,0},{2,3},{3,2},{4,5},{5,4},{6,7},{7,6},{8,9},{9,8},{10,11... | collective-permute-start | bytes 294920 | tf_op jit(solution)/shard_map/ppermute | solution.py:541
  23.1 1.3 %collective-permute-start.1 = (f32[192,128]{1,0:T(8,128)S(1)}, f32[192,128]{1,0:T(8,128)S(1)}, u32[]{:S(2)}, u32[]{:S(2)}) collective-permute-start(f32[192,128]{1,0:T(8,128)S(1)} %bitcast.32), channel_id=1, source_target_pairs={{0,1},{1,0},{2,3},{3,2},{4,5},{5,4},{6,7},{7,6},{8,9},{9,8},{10,11... | collective-permute-start | bytes 294920 | tf_op jit(solution)/shard_map/ppermute | solution.py:542
  24.2 0.6 copy-start.2
  24.8 0.6 copy-start.3
